TPU v7x, 128 devices: a whole 4x4x4 slice. The times are simulated.
128 devices in a mesh: fibre: 64 (over y_lo, z, x, core), freq: 2 (over y_hi).
Axes of the slice: x: 4, y: 4 (y_hi: 2, y_lo: 2; y = y_hi * 2 + y_lo), z: 4, core: 2. Of those that a mesh axis runs over, the one named last changes fastest.
Arguments:
- traces: bfloat16 [2, 4096, 4096], P(None, 'fibre'), may hold values from -50 to 50, as said below
- live: int32 [4096], P('fibre'), may hold values 0 or 1
- reach: int32 [64], P('fibre'), may hold values from 1 to 8
Outputs:
- correlations: float32 [64, 8, 64, 64, 128], P('fibre', 'freq')
Inputs may be any that keep to these rules, and one draw needn't show every extreme that they name: `traces`: records of the fibre's channels.
All inputs are finite; a program needn't handle non-finite values. No bound on the sum of `live` on one device may be relied on, other than what follows from the above.
Results may differ from a plain program's by a relative error of at most 0.0057.
Values may be sent and summed in bfloat16 or wider, within the bound.
A program may use at most 64 MiB of HBM per device.

v0:
```python
import math

import jax
import jax.numpy as jnp
from jax import lax
from jax.sharding import PartitionSpec as P

BAND = 64
OFF = 8
LAGS = 128


def from_behind(x, axis, by):
    peers = lax.axis_size(axis)
    pairs = [(i, i + by) for i in range(peers) if 0 <= i + by < peers]
    return lax.ppermute(x, axis, pairs)


def phase_angle(freq_ids, sample_ids, period):
    product = freq_ids[:, None] * sample_ids[None, :] % period
    return product.astype(jnp.float32) * (2.0 * math.pi / period)


def correlate(own_block, partner, first_freq, windows, channels, samples):
    freq_span = own_block.shape[2]
    block_width = math.gcd(freq_span, 256)
    own_split = own_block.reshape(2, windows, channels, freq_span)
    partner_split = partner.reshape(2, windows, channels, freq_span)
    lag_steps = jnp.arange(LAGS, dtype=jnp.int32) - LAGS // 2 + samples

    def accumulate(block_index, summed):
        first = block_index * block_width
        own_part = lax.dynamic_slice_in_dim(own_split, first, block_width, 3).astype(jnp.float32)
        partner_part = lax.dynamic_slice_in_dim(partner_split, first, block_width, 3).astype(
            jnp.float32
        )
        cross_real = (
            own_part[0][:, :, None, :] * partner_part[0][:, None, :, :]
            + own_part[1][:, :, None, :] * partner_part[1][:, None, :, :]
        ).sum(0)
        cross_imag = (
            own_part[1][:, :, None, :] * partner_part[0][:, None, :, :]
            - own_part[0][:, :, None, :] * partner_part[1][:, None, :, :]
        ).sum(0)
        cross_block = (
            jnp.stack([cross_real, cross_imag], axis=2)
            .astype(jnp.bfloat16)
            .reshape(channels * channels, 2 * block_width)
        )
        freq_ids = first_freq + first + jnp.arange(block_width, dtype=jnp.int32)
        angles = phase_angle(freq_ids, lag_steps, samples)
        lag_table = jnp.concatenate(
            [jnp.cos(angles).astype(jnp.bfloat16), (-jnp.sin(angles)).astype(jnp.bfloat16)]
        )
        return summed + jnp.dot(cross_block, lag_table, preferred_element_type=jnp.float32).reshape(
            channels, channels, LAGS
        )

    start_value = jnp.zeros((channels, channels, LAGS), jnp.float32)
    return lax.fori_loop(0, freq_span // block_width, accumulate, start_value)


def whiten_range(flat_rows, live, first_freq, span, windows, samples):
    row_count = flat_rows.shape[0]
    dft_width = math.gcd(span, 128)
    sample_ids = jnp.arange(samples, dtype=jnp.int32)

    def transform(block_index):
        freq_ids = first_freq + block_index * dft_width + jnp.arange(dft_width, dtype=jnp.int32)
        angles = phase_angle(freq_ids, sample_ids, samples)
        cosine = jnp.cos(angles).astype(jnp.bfloat16)
        sine_table = (-jnp.sin(angles)).astype(jnp.bfloat16)
        real_part = lax.dot_general(
            flat_rows, cosine, (((1,), (1,)), ((), ())), preferred_element_type=jnp.float32
        )
        imag_part = lax.dot_general(
            flat_rows, sine_table, (((1,), (1,)), ((), ())), preferred_element_type=jnp.float32
        )
        return jnp.stack([real_part, imag_part])

    blocks = lax.map(transform, jnp.arange(span // dft_width, dtype=jnp.int32))
    spectra = blocks.transpose(1, 2, 0, 3).reshape(2, row_count, span)
    band_power = (
        (spectra[0] * spectra[0] + spectra[1] * spectra[1])
        .reshape(row_count, span // BAND, BAND)
        .mean(-1)
    )
    whiten_gain = jnp.repeat(1.0 / jnp.sqrt(band_power + 1e-06), BAND, axis=1)
    alive_rows = jnp.tile(live.astype(jnp.float32), windows)
    return (spectra * whiten_gain[None] * alive_rows[None, :, None]).astype(jnp.bfloat16)


def per_device(traces, live, reach):
    windows, channels, samples = traces.shape
    row_count = windows * channels
    freq_count = samples // 2
    freq_groups = lax.axis_size("freq")
    local_freqs = freq_count // freq_groups
    band_index = lax.axis_index("freq")
    flat_rows = traces.reshape(row_count, samples)
    owned_offsets = OFF // freq_groups
    whitened = whiten_range(
        flat_rows, live, band_index * local_freqs, local_freqs, windows, samples
    )
    pieces = [whitened]
    for offset in range(1, OFF):
        pieces.append(from_behind(whitened, "fibre", -offset))
    partners = jnp.stack(pieces)
    own_whole = lax.all_gather(whitened, "freq", axis=2, tiled=True)
    my_partners = lax.all_to_all(partners, "freq", split_axis=0, concat_axis=3, tiled=True)
    result = lax.map(
        lambda partner: correlate(own_whole, partner, 0, windows, channels, samples), my_partners
    )
    offset_ids = band_index * owned_offsets + jnp.arange(owned_offsets, dtype=jnp.int32)
    keep_mask = (offset_ids < reach[0]).astype(jnp.float32)
    normal_scale = 1.0 / math.sqrt(windows * freq_count)
    return (result * normal_scale * keep_mask[:, None, None, None])[None]


def solution(mesh):
    placed = (P(None, "fibre", None), P("fibre"), P("fibre"))
    return jax.shard_map(
        per_device,
        mesh=mesh,
        in_specs=placed,
        out_specs=P("fibre", "freq", None, None, None),
        check_vma=False,
    )
```

profile of v0, /device:TPU:23, one launch (start us, length us, event | category | flops | bytes accessed | tf_op | source)
XLA Modules:
  0.0 744.2 jit_solution(6991338551533865801)
XLA Ops:
  6.5 148.9 %while.58 = (s32[]{:T(128)}, f32[8,2,128,128]{2,3,0,1:T(8,128)S(1)}, s32[8]{0:T(128)S(1)}, s32[]{:T(128)}, bf16[128,4096]{1,0:T(8,128)(2,1)}, /*index=5*/s32[]{:T(128)}, s32[1]{0:T(128)}) while((s32[]{:T(128)}, f32[8,2,128,128]{2,3,0,1:T(8,128)S(1)}, s32[8]{0:T(128)S(1)}, s32[]{:T(128)}, bf16[128,4096]{1,0:T(8,128)(2,1)}, ...), condition=%wide.region_1.2_spmd.clone, body=%wide.region_0.1_spmd.clone.sunk | while | flops 284721280 | bytes 6686357 | solution.py:81
  7.8 9.3 %convolution_bitcast_fusion.4 = f32[1,128,128]{1,2,0:T(8,128)S(1)} fusion(bf16[128,4096]{1,0:T(8,128)(2,1)} %get-tuple-element.554, s32[128]{0:T(128)S(1)} %iota_add_fusion.6), kind=kOutput, calls=%fused_computation.14.clone.1 | convolution fusion | flops 142606336 | bytes 1114624 | tf_op jit(solution)/shard_map/while/body/eval_jaxpr/dot_general | solution.py:76
  17.2 7.9 %convolution_bitcast_fusion.5 = f32[1,128,128]{1,2,0:T(8,128)S(1)} fusion(bf16[128,4096]{1,0:T(8,128)(2,1)S(1)} %copy-done.2, s32[128]{0:T(128)S(1)} %iota_add_fusion.6), kind=kOutput, calls=%fused_computation.15.clone.1 | convolution fusion | flops 142082048 | bytes 1114624 | tf_op jit(solution)/shard_map/while/body/eval_jaxpr/dot_general | solution.py:73
  26.4 9.3 %convolution_bitcast_fusion.4 = f32[1,128,128]{1,2,0:T(8,128)S(1)} fusion(bf16[128,4096]{1,0:T(8,128)(2,1)} %get-tuple-element.554, s32[128]{0:T(128)S(1)} %iota_add_fusion.6), kind=kOutput, calls=%fused_computation.14.clone.1 | convolution fusion | flops 142606336 | bytes 1114624 | tf_op jit(solution)/shard_map/while/body/eval_jaxpr/dot_general | solution.py:76
  35.8 7.9 %convolution_bitcast_fusion.5 = f32[1,128,128]{1,2,0:T(8,128)S(1)} fusion(bf16[128,4096]{1,0:T(8,128)(2,1)S(1)} %copy-done.2, s32[128]{0:T(128)S(1)} %iota_add_fusion.6), kind=kOutput, calls=%fused_computation.15.clone.1 | convolution fusion | flops 142082048 | bytes 1114624 | tf_op jit(solution)/shard_map/while/body/eval_jaxpr/dot_general | solution.py:73
  45.0 9.3 %convolution_bitcast_fusion.4 = f32[1,128,128]{1,2,0:T(8,128)S(1)} fusion(bf16[128,4096]{1,0:T(8,128)(2,1)} %get-tuple-element.554, s32[128]{0:T(128)S(1)} %iota_add_fusion.6), kind=kOutput, calls=%fused_computation.14.clone.1 | convolution fusion | flops 142606336 | bytes 1114624 | tf_op jit(solution)/shard_map/while/body/eval_jaxpr/dot_general | solution.py:76
  54.4 7.9 %convolution_bitcast_fusion.5 = f32[1,128,128]{1,2,0:T(8,128)S(1)} fusion(bf16[128,4096]{1,0:T(8,128)(2,1)S(1)} %copy-done.2, s32[128]{0:T(128)S(1)} %iota_add_fusion.6), kind=kOutput, calls=%fused_computation.15.clone.1 | convolution fusion | flops 142082048 | bytes 1114624 | tf_op jit(solution)/shard_map/while/body/eval_jaxpr/dot_general | solution.py:73
  63.6 9.3 %convolution_bitcast_fusion.4 = f32[1,128,128]{1,2,0:T(8,128)S(1)} fusion(bf16[128,4096]{1,0:T(8,128)(2,1)} %get-tuple-element.554, s32[128]{0:T(128)S(1)} %iota_add_fusion.6), kind=kOutput, calls=%fused_computation.14.clone.1 | convolution fusion | flops 142606336 | bytes 1114624 | tf_op jit(solution)/shard_map/while/body/eval_jaxpr/dot_general | solution.py:76
  73.0 7.9 %convolution_bitcast_fusion.5 = f32[1,128,128]{1,2,0:T(8,128)S(1)} fusion(bf16[128,4096]{1,0:T(8,128)(2,1)S(1)} %copy-done.2, s32[128]{0:T(128)S(1)} %iota_add_fusion.6), kind=kOutput, calls=%fused_computation.15.clone.1 | convolution fusion | flops 142082048 | bytes 1114624 | tf_op jit(solution)/shard_map/while/body/eval_jaxpr/dot_general | solution.py:73
  82.2 9.3 %convolution_bitcast_fusion.4 = f32[1,128,128]{1,2,0:T(8,128)S(1)} fusion(bf16[128,4096]{1,0:T(8,128)(2,1)} %get-tuple-element.554, s32[128]{0:T(128)S(1)} %iota_add_fusion.6), kind=kOutput, calls=%fused_computation.14.clone.1 | convolution fusion | flops 142606336 | bytes 1114624 | tf_op jit(solution)/shard_map/while/body/eval_jaxpr/dot_general | solution.py:76
  91.6 7.9 %convolution_bitcast_fusion.5 = f32[1,128,128]{1,2,0:T(8,128)S(1)} fusion(bf16[128,4096]{1,0:T(8,128)(2,1)S(1)} %copy-done.2, s32[128]{0:T(128)S(1)} %iota_add_fusion.6), kind=kOutput, calls=%fused_computation.15.clone.1 | convolution fusion | flops 142082048 | bytes 1114624 | tf_op jit(solution)/shard_map/while/body/eval_jaxpr/dot_general | solution.py:73
  100.8 9.3 %convolution_bitcast_fusion.4 = f32[1,128,128]{1,2,0:T(8,128)S(1)} fusion(bf16[128,4096]{1,0:T(8,128)(2,1)} %get-tuple-element.554, s32[128]{0:T(128)S(1)} %iota_add_fusion.6), kind=kOutput, calls=%fused_computation.14.clone.1 | convolution fusion | flops 142606336 | bytes 1114624 | tf_op jit(solution)/shard_map/while/body/eval_jaxpr/dot_general | solution.py:76
  110.1 7.9 %convolution_bitcast_fusion.5 = f32[1,128,128]{1,2,0:T(8,128)S(1)} fusion(bf16[128,4096]{1,0:T(8,128)(2,1)S(1)} %copy-done.2, s32[128]{0:T(128)S(1)} %iota_add_fusion.6), kind=kOutput, calls=%fused_computation.15.clone.1 | convolution fusion | flops 142082048 | bytes 1114624 | tf_op jit(solution)/shard_map/while/body/eval_jaxpr/dot_general | solution.py:73
  119.4 9.3 %convolution_bitcast_fusion.4 = f32[1,128,128]{1,2,0:T(8,128)S(1)} fusion(bf16[128,4096]{1,0:T(8,128)(2,1)} %get-tuple-element.554, s32[128]{0:T(128)S(1)} %iota_add_fusion.6), kind=kOutput, calls=%fused_computation.14.clone.1 | convolution fusion | flops 142606336 | bytes 1114624 | tf_op jit(solution)/shard_map/while/body/eval_jaxpr/dot_general | solution.py:76
  128.7 7.9 %convolution_bitcast_fusion.5 = f32[1,128,128]{1,2,0:T(8,128)S(1)} fusion(bf16[128,4096]{1,0:T(8,128)(2,1)S(1)} %copy-done.2, s32[128]{0:T(128)S(1)} %iota_add_fusion.6), kind=kOutput, calls=%fused_computation.15.clone.1 | convolution fusion | flops 142082048 | bytes 1114624 | tf_op jit(solution)/shard_map/while/body/eval_jaxpr/dot_general | solution.py:73
  138.0 9.3 %convolution_bitcast_fusion.4 = f32[1,128,128]{1,2,0:T(8,128)S(1)} fusion(bf16[128,4096]{1,0:T(8,128)(2,1)} %get-tuple-element.554, s32[128]{0:T(128)S(1)} %iota_add_fusion.6), kind=kOutput, calls=%fused_computation.14.clone.1 | convolution fusion | flops 142606336 | bytes 1114624 | tf_op jit(solution)/shard_map/while/body/eval_jaxpr/dot_general | solution.py:76
  147.3 7.9 %convolution_bitcast_fusion.5 = f32[1,128,128]{1,2,0:T(8,128)S(1)} fusion(bf16[128,4096]{1,0:T(8,128)(2,1)S(1)} %copy-done.2, s32[128]{0:T(128)S(1)} %iota_add_fusion.6), kind=kOutput, calls=%fused_computation.15.clone.1 | convolution fusion | flops 142082048 | bytes 1114624 | tf_op jit(solution)/shard_map/while/body/eval_jaxpr/dot_general | solution.py:73
  176.4 7.5 %collective-permute-start.6 = (bf16[2,128,1024]{1,2,0:T(8,128)(2,1)S(1)}, bf16[2,128,1024]{1,2,0:T(8,128)(2,1)S(1)}, u32[]{:S(2)}, u32[]{:S(2)}) collective-permute-start(bf16[2,128,1024]{1,2,0:T(8,128)(2,1)S(1)} %fusion.30), channel_id=1, source_target_pairs={{14,0},{16,2},{18,4},{20,6},{22,8},{24,10},{26,12},{28,14},{30,16}... | collective-permute-start | bytes 1572872 | tf_op jit(solution)/shard_map/ppermute | solution.py:16
  184.8 12.2 %collective-permute-done.2 = bf16[2,128,1024]{1,2,0:T(8,128)(2,1)S(1)} collective-permute-done((bf16[2,128,1024]{1,2,0:T(8,128)(2,1)S(1)}, bf16[2,128,1024]{1,2,0:T(8,128)(2,1)S(1)}, u32[]{:S(2)}, u32[]{:S(2)}) %collective-permute-start.2) | collective-permute-done | bytes 524320 | tf_op jit(solution)/shard_map/ppermute | solution.py:16
  197.9 5.5 collective-permute-done.3
  204.2 9.2 %collective-permute-done.4 = bf16[2,128,1024]{1,2,0:T(8,128)(2,1)S(1)} collective-permute-done((bf16[2,128,1024]{1,2,0:T(8,128)(2,1)S(1)}, bf16[2,128,1024]{1,2,0:T(8,128)(2,1)S(1)}, u32[]{:S(2)}, u32[]{:S(2)}) %collective-permute-start.4) | collective-permute-done | bytes 524320 | tf_op jit(solution)/shard_map/ppermute | solution.py:16
  214.2 7.2 collective-permute-done.5
  222.3 13.6 %collective-permute-done.6 = bf16[2,128,1024]{1,2,0:T(8,128)(2,1)S(1)} collective-permute-done((bf16[2,128,1024]{1,2,0:T(8,128)(2,1)S(1)}, bf16[2,128,1024]{1,2,0:T(8,128)(2,1)S(1)}, u32[]{:S(2)}, u32[]{:S(2)}) %collective-permute-start.6) | collective-permute-done | bytes 524320 | tf_op jit(solution)/shard_map/ppermute | solution.py:16
  236.8 5.6 all-to-all-start
  244.4 38.2 %all-gather.2.cloned.1.call-done = bf16[2,128,2048]{1,2,0:T(8,128)(2,1)} async-done(((bf16[2,128,1024]{1,2,0:T(8,128)(2,1)}), bf16[2,128,2048]{1,2,0:T(8,128)(2,1)}) %all-gather.2.cloned.1.call-update) | async-done | bytes 1048592 | tf_op jit(solution)/shard_map/all_gather | solution.py:109
  284.9 10.4 %all-to-all-done = bf16[8,2,128,1024]{2,3,1,0:T(8,128)(2,1)} async-done(((bf16[8,2,128,1024]{2,3,1,0:T(8,128)(2,1)}), bf16[8,2,128,1024]{2,3,1,0:T(8,128)(2,1)}, u32[]{:S(2)}, u32[]{:S(2)}) %all-to-all-start) | async-done | bytes 4194336 | tf_op jit(solution)/shard_map/all_to_all | solution.py:110
  295.2 11.2 %copy.11 = bf16[4,2,128,2,1024]{4,3,2,1,0:T(2,128)(2,1)} copy(bf16[4,2,128,2,1024]{2,4,1,0,3:T(8,128)(2,1)} %bitcast.17) | data formatting | bytes 8388608 | tf_op jit(solution)/shard_map/all_to_all | solution.py:110
  306.5 7.8 %all_to_all.16 = bf16[4,2,128,2048]{3,2,1,0:T(8,128)(2,1)} reshape(bf16[4,2,128,2,1024]{4,3,2,1,0:T(2,128)(2,1)} %copy.11) | data formatting | bytes 8388608 | tf_op jit(solution)/shard_map/all_to_all | solution.py:110
  314.2 414.4 %while.57 = (s32[]{:T(128)}, f32[4,64,64,128]{3,2,1,0:T(8,128)}, bf16[2,128,2048]{2,1,0:T(8,128)(2,1)}, bf16[4,2,128,2048]{3,2,1,0:T(8,128)(2,1)}, s32[]{:T(128)...) while((s32[]{:T(128)}, f32[4,64,64,128]{3,2,1,0:T(8,128)}, ...), condition=%wide.region_8.9_spmd, body=%wide.region_3.8_spmd.sunk | while | flops 555647360 | bytes 38276932 | solution.py:111
  315.5 100.8 %while.59 = (s32[]{:T(128)}, f32[64,64,128]{2,1,0:T(8,128)S(1)}, bf16[2,2,64,2048]{3,2,1,0:T(8,128)(2,1)}, bf16[2,2,64,2048]{3,2,1,0:T(8,128)(2,1)S(1)}, s32[]{:T(128)}, /*index=5*/s32[]{:T(128)}, s32[]{:T(128)}, s32[]{:T(128)}) while((s32[]{:T(128)}, f32[64,64,128]{2,1,0:T(8,128)S(1)}, bf16[2,2,64,2048]{3,2,1,0:T(8,128)(2,1)}, ...), condition=%wide.region_7.7_spmd.clone, body=%wide.region_4.6_spmd.clone.sunk | while | flops 555647360 | bytes 31984788 | solution.py:60
  316.6 4.6 add_reduce_fusion.2
  329.2 4.6 add_reduce_fusion.2
  341.8 4.6 add_reduce_fusion.2
  354.4 4.6 add_reduce_fusion.2
  367.0 4.6 add_reduce_fusion.2
  379.6 4.6 add_reduce_fusion.2
  392.2 4.6 add_reduce_fusion.2
  404.8 4.6 add_reduce_fusion.2
  419.1 100.8 %while.59 = (s32[]{:T(128)}, f32[64,64,128]{2,1,0:T(8,128)S(1)}, bf16[2,2,64,2048]{3,2,1,0:T(8,128)(2,1)}, bf16[2,2,64,2048]{3,2,1,0:T(8,128)(2,1)S(1)}, s32[]{:T(128)}, /*index=5*/s32[]{:T(128)}, s32[]{:T(128)}, s32[]{:T(128)}) while((s32[]{:T(128)}, f32[64,64,128]{2,1,0:T(8,128)S(1)}, bf16[2,2,64,2048]{3,2,1,0:T(8,128)(2,1)}, ...), condition=%wide.region_7.7_spmd.clone, body=%wide.region_4.6_spmd.clone.sunk | while | flops 555647360 | bytes 31984788 | solution.py:60
  420.2 4.6 add_reduce_fusion.2
  432.8 4.6 add_reduce_fusion.2
  445.4 4.6 add_reduce_fusion.2
  458.0 4.6 add_reduce_fusion.2
  470.6 4.6 add_reduce_fusion.2
  483.2 4.6 add_reduce_fusion.2
  495.8 4.6 add_reduce_fusion.2
  508.4 4.6 add_reduce_fusion.2
  522.7 100.8 %while.59 = (s32[]{:T(128)}, f32[64,64,128]{2,1,0:T(8,128)S(1)}, bf16[2,2,64,2048]{3,2,1,0:T(8,128)(2,1)}, bf16[2,2,64,2048]{3,2,1,0:T(8,128)(2,1)S(1)}, s32[]{:T(128)}, /*index=5*/s32[]{:T(128)}, s32[]{:T(128)}, s32[]{:T(128)}) while((s32[]{:T(128)}, f32[64,64,128]{2,1,0:T(8,128)S(1)}, bf16[2,2,64,2048]{3,2,1,0:T(8,128)(2,1)}, ...), condition=%wide.region_7.7_spmd.clone, body=%wide.region_4.6_spmd.clone.sunk | while | flops 555647360 | bytes 31984788 | solution.py:60
  523.7 4.6 add_reduce_fusion.2
  536.3 4.6 add_reduce_fusion.2
  549.0 4.6 add_reduce_fusion.2
  561.6 4.6 add_reduce_fusion.2
  574.1 4.6 add_reduce_fusion.2
  586.8 4.6 add_reduce_fusion.2
  599.4 4.6 add_reduce_fusion.2
  612.0 4.6 add_reduce_fusion.2
  626.3 100.8 %while.59 = (s32[]{:T(128)}, f32[64,64,128]{2,1,0:T(8,128)S(1)}, bf16[2,2,64,2048]{3,2,1,0:T(8,128)(2,1)}, bf16[2,2,64,2048]{3,2,1,0:T(8,128)(2,1)S(1)}, s32[]{:T(128)}, /*index=5*/s32[]{:T(128)}, s32[]{:T(128)}, s32[]{:T(128)}) while((s32[]{:T(128)}, f32[64,64,128]{2,1,0:T(8,128)S(1)}, bf16[2,2,64,2048]{3,2,1,0:T(8,128)(2,1)}, ...), condition=%wide.region_7.7_spmd.clone, body=%wide.region_4.6_spmd.clone.sunk | while | flops 555647360 | bytes 31984788 | solution.py:60
  627.3 4.6 add_reduce_fusion.2
  639.9 4.6 add_reduce_fusion.2
  652.5 4.6 add_reduce_fusion.2
  665.1 4.6 add_reduce_fusion.2
  677.7 4.6 add_reduce_fusion.2
  690.3 4.6 add_reduce_fusion.2
  728.6 8.7 %multiply_bitcast_fusion = f32[1,4,64,64,128]{4,3,2,1,0:T(8,128)} fusion(f32[4,64,64,128]{3,2,1,0:T(8,128)} %get-tuple-element.326, f32[4]{0:T(128)S(1)} %copy-done.1), kind=kLoop, calls=%fused_computation.57 | loop fusion | flops 2097152 | bytes 16777232 | tf_op jit(solution)/shard_map/broadcast_in_dim | solution.py:117
  (379 shorter events, 309.6 us)
Async XLA Ops:
  6.5 149.1 %copy-start.3 = (s32[64]{0:T(128)S(1)}, s32[64]{0:T(128)}, u32[]{:S(2)}) copy-start(s32[64]{0:T(128)} %param.10) | copy-start | bytes 772
  7.8 9.4 %copy-start.2 = (bf16[128,4096]{1,0:T(8,128)(2,1)S(1)}, bf16[128,4096]{1,0:T(8,128)(2,1)}, u32[]{:S(2)}) copy-start(bf16[128,4096]{1,0:T(8,128)(2,1)} %get-tuple-element.554) | copy-start | bytes 3145732 | tf_op jit(solution)/shard_map/while
  26.4 9.4 %copy-start.2 = (bf16[128,4096]{1,0:T(8,128)(2,1)S(1)}, bf16[128,4096]{1,0:T(8,128)(2,1)}, u32[]{:S(2)}) copy-start(bf16[128,4096]{1,0:T(8,128)(2,1)} %get-tuple-element.554) | copy-start | bytes 3145732 | tf_op jit(solution)/shard_map/while
  45.0 9.4 %copy-start.2 = (bf16[128,4096]{1,0:T(8,128)(2,1)S(1)}, bf16[128,4096]{1,0:T(8,128)(2,1)}, u32[]{:S(2)}) copy-start(bf16[128,4096]{1,0:T(8,128)(2,1)} %get-tuple-element.554) | copy-start | bytes 3145732 | tf_op jit(solution)/shard_map/while
  63.6 9.4 %copy-start.2 = (bf16[128,4096]{1,0:T(8,128)(2,1)S(1)}, bf16[128,4096]{1,0:T(8,128)(2,1)}, u32[]{:S(2)}) copy-start(bf16[128,4096]{1,0:T(8,128)(2,1)} %get-tuple-element.554) | copy-start | bytes 3145732 | tf_op jit(solution)/shard_map/while
  82.2 9.4 %copy-start.2 = (bf16[128,4096]{1,0:T(8,128)(2,1)S(1)}, bf16[128,4096]{1,0:T(8,128)(2,1)}, u32[]{:S(2)}) copy-start(bf16[128,4096]{1,0:T(8,128)(2,1)} %get-tuple-element.554) | copy-start | bytes 3145732 | tf_op jit(solution)/shard_map/while
  100.8 9.4 %copy-start.2 = (bf16[128,4096]{1,0:T(8,128)(2,1)S(1)}, bf16[128,4096]{1,0:T(8,128)(2,1)}, u32[]{:S(2)}) copy-start(bf16[128,4096]{1,0:T(8,128)(2,1)} %get-tuple-element.554) | copy-start | bytes 3145732 | tf_op jit(solution)/shard_map/while
  119.4 9.4 %copy-start.2 = (bf16[128,4096]{1,0:T(8,128)(2,1)S(1)}, bf16[128,4096]{1,0:T(8,128)(2,1)}, u32[]{:S(2)}) copy-start(bf16[128,4096]{1,0:T(8,128)(2,1)} %get-tuple-element.554) | copy-start | bytes 3145732 | tf_op jit(solution)/shard_map/while
  138.0 9.4 %copy-start.2 = (bf16[128,4096]{1,0:T(8,128)(2,1)S(1)}, bf16[128,4096]{1,0:T(8,128)(2,1)}, u32[]{:S(2)}) copy-start(bf16[128,4096]{1,0:T(8,128)(2,1)} %get-tuple-element.554) | copy-start | bytes 3145732 | tf_op jit(solution)/shard_map/while
  155.9 66.4 %copy-start = (bf16[2,128,1024]{1,2,0:T(8,128)(2,1)}, bf16[2,128,1024]{1,2,0:T(8,128)(2,1)S(1)}, u32[]{:S(2)}) copy-start(bf16[2,128,1024]{1,2,0:T(8,128)(2,1)S(1)} %fusion.30) | copy-start | bytes 1572868
  155.9 16.2 %collective-permute-start = (bf16[2,128,1024]{1,2,0:T(8,128)(2,1)S(1)}, bf16[2,128,1024]{1,2,0:T(8,128)(2,1)S(1)}, u32[]{:S(2)}, u32[]{:S(2)}) collective-permute-start(bf16[2,128,1024]{1,2,0:T(8,128)(2,1)S(1)} %fusion.30), channel_id=1, source_target_pairs={{2,0},{4,2},{6,4},{8,6},{10,8},{12,10},{14,12},{16,14},{18,16},{20... | collective-permute-start | bytes 1572872 | tf_op jit(solution)/shard_map/ppermute | solution.py:16
  158.5 17.9 %collective-permute-start.1 = (bf16[2,128,1024]{1,2,0:T(8,128)(2,1)S(1)}, bf16[2,128,1024]{1,2,0:T(8,128)(2,1)S(1)}, u32[]{:S(2)}, u32[]{:S(2)}) collective-permute-start(bf16[2,128,1024]{1,2,0:T(8,128)(2,1)S(1)} %fusion.30), channel_id=1, source_target_pairs={{4,0},{6,2},{8,4},{10,6},{12,8},{14,10},{16,12},{18,14},{20,16},{2... | collective-permute-start | bytes 1572872 | tf_op jit(solution)/shard_map/ppermute | solution.py:16
  160.9 36.1 %collective-permute-start.2 = (bf16[2,128,1024]{1,2,0:T(8,128)(2,1)S(1)}, bf16[2,128,1024]{1,2,0:T(8,128)(2,1)S(1)}, u32[]{:S(2)}, u32[]{:S(2)}) collective-permute-start(bf16[2,128,1024]{1,2,0:T(8,128)(2,1)S(1)} %fusion.30), channel_id=1, source_target_pairs={{6,0},{8,2},{10,4},{12,6},{14,8},{16,10},{18,12},{20,14},{22,16},{... | collective-permute-start | bytes 1572872 | tf_op jit(solution)/shard_map/ppermute | solution.py:16
  163.3 40.1 %collective-permute-start.3 = (bf16[2,128,1024]{1,2,0:T(8,128)(2,1)S(1)}, bf16[2,128,1024]{1,2,0:T(8,128)(2,1)S(1)}, u32[]{:S(2)}, u32[]{:S(2)}) collective-permute-start(bf16[2,128,1024]{1,2,0:T(8,128)(2,1)S(1)} %fusion.30), channel_id=1, source_target_pairs={{8,0},{10,2},{12,4},{14,6},{16,8},{18,10},{20,12},{22,14},{24,16},... | collective-permute-start | bytes 1572872 | tf_op jit(solution)/shard_map/ppermute | solution.py:16
  165.6 47.8 %collective-permute-start.4 = (bf16[2,128,1024]{1,2,0:T(8,128)(2,1)S(1)}, bf16[2,128,1024]{1,2,0:T(8,128)(2,1)S(1)}, u32[]{:S(2)}, u32[]{:S(2)}) collective-permute-start(bf16[2,128,1024]{1,2,0:T(8,128)(2,1)S(1)} %fusion.30), channel_id=1, source_target_pairs={{10,0},{12,2},{14,4},{16,6},{18,8},{20,10},{22,12},{24,14},{26,16}... | collective-permute-start | bytes 1572872 | tf_op jit(solution)/shard_map/ppermute | solution.py:16
  172.1 49.4 %collective-permute-start.5 = (bf16[2,128,1024]{1,2,0:T(8,128)(2,1)S(1)}, bf16[2,128,1024]{1,2,0:T(8,128)(2,1)S(1)}, u32[]{:S(2)}, u32[]{:S(2)}) collective-permute-start(bf16[2,128,1024]{1,2,0:T(8,128)(2,1)S(1)} %fusion.30), channel_id=1, source_target_pairs={{12,0},{14,2},{16,4},{18,6},{20,8},{22,10},{24,12},{26,14},{28,16}... | collective-permute-start | bytes 1572872 | tf_op jit(solution)/shard_map/ppermute | solution.py:16
  176.4 59.5 %collective-permute-start.6 = (bf16[2,128,1024]{1,2,0:T(8,128)(2,1)S(1)}, bf16[2,128,1024]{1,2,0:T(8,128)(2,1)S(1)}, u32[]{:S(2)}, u32[]{:S(2)}) collective-permute-start(bf16[2,128,1024]{1,2,0:T(8,128)(2,1)S(1)} %fusion.30), channel_id=1, source_target_pairs={{14,0},{16,2},{18,4},{20,6},{22,8},{24,10},{26,12},{28,14},{30,16}... | collective-permute-start | bytes 1572872 | tf_op jit(solution)/shard_map/ppermute | solution.py:16
  236.8 58.4 %all-to-all-start = ((bf16[8,2,128,1024]{2,3,1,0:T(8,128)(2,1)}), bf16[8,2,128,1024]{2,3,1,0:T(8,128)(2,1)}, u32[]{:S(2)}, u32[]{:S(2)}) async-start(bf16[8,2,128,1024]{2,3,1,0:T(8,128)(2,1)} %bitcast_dynamic-update-slice_fusion.1), calls=%async_computation | async-start | bytes 8388608 | tf_op jit(solution)/shard_map/all_to_all | solution.py:110
  242.4 40.1 %all-gather.2.cloned.1.call-start = ((), (), s32[]{:S(2)}) async-start(), calls=%async_computation.1 | async-start | bytes 1572864 | tf_op jit(solution)/shard_map/all_gather | solution.py:109
  314.2 414.4 %copy-start.1 = (f32[4]{0:T(128)S(1)}, f32[4]{0:T(128)}, u32[]{:S(2)}) copy-start(f32[4]{0:T(128)} %compare_select_fusion) | copy-start | bytes 52
Sparse Core Ops, SparseCore 0:
  244.9 37.6 all-gather.1
where the time goes:
time: 755 us; the launch traced here: 744 us
  matrix products  254 us (34%)
  other arithmetic  219 us (29%)
  local copies, waits for them, and re-layouts  120 us (16%)
  waiting for transfers between devices  102 us (14%)
  starting transfers between devices  26.7 us (4%)
  between operations  14.2 us (2%)
  loops' own time  8.27 us (1%)
    reduce_sum x32, other arithmetic, accumulate(): cross_real = (own_part[0][:, :, None, :] * partner_part[0][:, None, :, :]...  146 us
    dot_general x32, matrix products, accumulate(): jnp.dot(cross_block, lag_table, preferred_element_type=jnp.float32)  116 us
    convert_element_type x32, local copies, waits for them, and re-layouts, accumulate(): cross_block = jnp.stack([cross_real, cross_imag], axis=2).astype(jnp.bflo...  75.5 us
    dot_general x8, matrix products, transform(): lax.dot_general(flat_rows, sine_table, (((1,), (1,)), ((), ())), preferre...  74.8 us
    dot_general x8, matrix products, transform(): lax.dot_general(flat_rows, cosine, (((1,), (1,)), ((), ())), preferred_el...  63.3 us
    ppermute x7, waiting for transfers between devices, from_behind(): return lax.ppermute(x, axis, pairs)  52.9 us
    all_gather x1, waiting for transfers between devices, per_device(): own_whole = lax.all_gather(whitened, 'freq', axis=2, tiled=True)  38.2 us
    convert_element_type x32, other arithmetic, accumulate(): lax.dynamic_slice_in_dim(partner_split, first, block_width, 3)  30.3 us
  transfers between devices with their start and end apart: 9, of which 9 were waited for; matrix products, arithmetic and copies ran while one was open for 1% of the time, Pallas kernels for 0%

commit v1 on v0

v1 whole, which is shorter than its diff:
```python
import functools
import math

import jax
import jax.numpy as jnp
import numpy as np
from jax import lax
from jax.experimental import pallas as pl
from jax.experimental.pallas import tpu as pltpu
from jax.sharding import PartitionSpec as P

BAND = 64
OFF = 8
LAGS = 128
F32 = jnp.float32
BF16 = jnp.bfloat16
NT = (((1,), (1,)), ((), ()))


def split_bf16(a):
    hi = a.astype(BF16)
    return hi, (a - hi.astype(F32)).astype(BF16)


def np_split(a):
    import ml_dtypes

    hi = a.astype(np.float32).astype(ml_dtypes.bfloat16)
    lo = (a - hi.astype(np.float64)).astype(np.float32).astype(ml_dtypes.bfloat16)
    return hi, lo


def make_tables():
    l = np.arange(128)
    ang = 2 * np.pi * (np.outer(l, l) % 128) / 128
    fwd = np.concatenate([np.cos(ang), -np.sin(ang)], 1)
    inv = np.concatenate([np.cos(ang), -np.sin(ang)], 0)
    fh, fl = np_split(fwd)
    ih, il = np_split(inv)
    e_fwd = np.concatenate([fh, fl], 0)
    e_inv = np.concatenate([ih, il], 1)
    band = (l[:, None] // BAND == l[None, :] // BAND).astype(np.float32)
    e_band = np.concatenate([band, band], 0).astype(fh.dtype)
    tw = 2 * np.pi * np.outer(np.arange(32), l) / 4096
    twid = np.stack([np.cos(tw), np.sin(tw)]).astype(np.float32)
    return e_fwd, e_inv, e_band, twid


def cadd(a, b):
    return a[0] + b[0], a[1] + b[1]


def csub(a, b):
    return a[0] - b[0], a[1] - b[1]


def cmul_i(a, sign):
    return (-a[1], a[0]) if sign > 0 else (a[1], -a[0])


def crot(a, num, den, sign):
    num %= den
    if num == 0:
        return a
    if 4 * num == den:
        return cmul_i(a, sign)
    if 2 * num == den:
        return -a[0], -a[1]
    if 4 * num == 3 * den:
        return cmul_i(a, -sign)
    if 8 * num % den == 0:
        h = math.sqrt(0.5)
        c = math.copysign(h, math.cos(2 * math.pi * num / den))
        s = sign * math.copysign(h, math.sin(2 * math.pi * num / den))
        if c > 0 and s > 0:
            return (a[0] - a[1]) * h, (a[0] + a[1]) * h
        if c > 0:
            return (a[0] + a[1]) * h, (a[1] - a[0]) * h
        if s > 0:
            return (a[0] + a[1]) * -h, (a[0] - a[1]) * h
        return (a[1] - a[0]) * h, (a[0] + a[1]) * -h
    c = math.cos(2 * math.pi * num / den)
    s = sign * math.sin(2 * math.pi * num / den)
    return a[0] * c - a[1] * s, a[0] * s + a[1] * c


def cfft(xs, sign):
    n = len(xs)
    if n == 1:
        return xs
    half = n // 2
    even = cfft([cadd(xs[i], xs[i + half]) for i in range(half)], sign)
    odd = cfft([crot(csub(xs[i], xs[i + half]), i, n, sign) for i in range(half)], sign)
    out = [None] * n
    out[0::2] = even
    out[1::2] = odd
    return out


def rfft_bins(xs):
    n = len(xs)
    if n == 1:
        return {0: (xs[0], None)}
    half = n // 2
    if xs[half] is None:
        e = d = xs[:half]
    else:
        e = [xs[i] + xs[i + half] for i in range(half)]
        d = [xs[i] - xs[i + half] for i in range(half)]
    out = {2 * k: v for k, v in rfft_bins(e).items()}
    if n == 2:
        out[1] = (d[0], None)
        return out
    q = n // 4
    z = [crot((d[s], -d[s + q]), s, n, -1) for s in range(q)]
    z = cfft(z, -1)
    for v in range(q):
        k = 4 * v + 1
        if k <= half:
            out[k] = z[v]
        else:
            out[n - k] = (z[v][0], -z[v][1])
    return out


def irfft_real(bins, n, keep_half=False):
    if n == 1:
        return [bins[0][0]]
    half = n // 2
    e = irfft_real({k // 2: v for k, v in bins.items() if k % 2 == 0}, half)
    if n == 2:
        d = [bins[1][0]]
    else:
        q = n // 4
        z = []
        for v in range(q):
            k = 4 * v + 1
            if k <= half:
                z.append(bins[k])
            else:
                re, im = bins[n - k]
                z.append((re, -im))
        z = cfft(z, 1)
        y = [crot(z[s], s, n, 1) for s in range(q)]
        d = [v[0] for v in y] + [-v[1] for v in y]
    lower = [e[i] + d[i] for i in range(half)]
    if keep_half:
        return lower
    return lower + [e[i] - d[i] for i in range(half)]


def whiten_to_time(x, live, e_fwd, e_inv, e_band, twid, r, xt, z, spec, pw, yh):
    def tr(q, _):
        col = pl.ds(pl.multiple_of(q * 128, 128), 128)
        for w in range(2):
            part = x[w, :, col].astype(F32)
            xt[col, w * 64 : w * 64 + 64] = part.T
        return 0

    lax.fori_loop(0, 32, tr, 0)

    def dft_l(s, _):
        v = xt[pl.ds(s, 128, stride=32), :].T.astype(BF16)
        g = jnp.dot(jnp.concatenate([v, v], 1), e_fwd[...], preferred_element_type=F32)
        z[0, s] = g[:, :128]
        z[1, s] = g[:, 128:]
        return 0

    lax.fori_loop(0, 32, dft_l, 0)

    def fwd(g, _):
        rows = pl.ds(pl.multiple_of(g * 8, 8), 8)
        for s0 in range(8):
            vals = []
            for s1 in range(4):
                s = 8 * s1 + s0
                a = z[0, s, rows], z[1, s, rows]
                if s:
                    c, n = twid[0, s : s + 1], twid[1, s : s + 1]
                    a = a[0] * c + a[1] * n, a[1] * c - a[0] * n
                vals.append(a)
            vals = cfft(vals, -1)
            for f0 in range(4):
                a = crot(vals[f0], f0 * s0, 32, -1)
                z[0, 8 * f0 + s0, rows], z[1, 8 * f0 + s0, rows] = a
        for f0 in range(4):
            vals = [(z[0, 8 * f0 + s0, rows], z[1, 8 * f0 + s0, rows]) for s0 in range(8)]
            vals = cfft(vals, -1)
            for f1 in range(4):
                f = 4 * f1 + f0
                spec[0, f, rows], spec[1, f, rows] = vals[f1]
                pw[f, rows] = vals[f1][0] * vals[f1][0] + vals[f1][1] * vals[f1][1]
        return 0

    lax.fori_loop(0, 16, fwd, 0)

    alive = jnp.concatenate([live[...], live[...]], 1).astype(F32)
    alive = jnp.broadcast_to(alive, (128, 128)).T * 2.0**-8
    lane = lax.broadcasted_iota(jnp.int32, (128, 128), 1)

    def band_gain(f, _):
        hi, lo = split_bf16(pw[f])
        bp = jnp.dot(jnp.concatenate([hi, lo], 1), e_band[...], preferred_element_type=F32)
        gain = lax.rsqrt(bp * (1.0 / BAND) + 1e-6) * alive
        pw[f] = jnp.where((lane == 0) & (f == 0), gain * math.sqrt(0.5), gain)
        return 0

    lax.fori_loop(0, 16, band_gain, 0)

    def inv(g, _):
        rows = pl.ds(pl.multiple_of(g * 8, 8), 8)
        for f0 in range(4):
            vals = []
            for f1 in range(4):
                f = 4 * f1 + f0
                k = pw[f, rows]
                vals.append((spec[0, f, rows] * k, spec[1, f, rows] * k))
            even = cfft(vals, 1)
            odd = cfft([crot(vals[i], i, 8, 1) for i in range(4)], 1)
            for s0 in range(8):
                a = (even if s0 % 2 == 0 else odd)[s0 // 2]
                a = crot(a, f0 * s0, 32, 1)
                z[0, 8 * f0 + s0, rows], z[1, 8 * f0 + s0, rows] = a
        for s0 in range(8):
            vals = [(z[0, 8 * f0 + s0, rows], z[1, 8 * f0 + s0, rows]) for f0 in range(4)]
            vals = cfft(vals, 1)
            for s1 in range(4):
                s = 8 * s1 + s0
                a = vals[s1]
                if s:
                    c, n = twid[0, s : s + 1], twid[1, s : s + 1]
                    a = a[0] * c - a[1] * n, a[1] * c + a[0] * n
                z[0, s, rows], z[1, s, rows] = a
        return 0

    lax.fori_loop(0, 16, inv, 0)

    def idft_l(s, _):
        both = jnp.concatenate([z[0, s], z[1, s]], 1)
        hi, lo = split_bf16(both)
        d = jnp.dot(jnp.concatenate([hi, lo], 0), e_inv[...], preferred_element_type=F32)
        d = d[:, :128] + d[:, 128:]
        d = (d[:128] + d[128:]).astype(BF16)
        r[s, :, 0:128] = d[:64]
        r[s, :, 128:256] = d[64:]
        return 0

    lax.fori_loop(0, 32, idft_l, 0)


def prepare_own(r, lhs, lhs0):
    def cols(g, _):
        rows = pl.ds(pl.multiple_of(g * 16, 16), 16)
        for h in range(2):
            lanes = slice(128 * h, 128 * h + 128)
            spectra = []
            for n0 in range(2):
                vals = []
                for n1 in range(16):
                    vals.append(r[2 * n1 + n0, rows, lanes].astype(F32))
                vals += [pltpu.roll(v, 127, 1) for v in vals]
                spectra.append(rfft_bins(vals))
            b0, b1 = spectra
            for e, k in enumerate((0, 16)):
                sgn = 1.0 if k == 0 else -1.0
                q0, q1, q2 = b0[k][0], b1[k][0], b0[k][0] * sgn
                for k0, pair in enumerate(((q0, q1), (q1, q2))):
                    for s0 in range(2):
                        at = pl.ds(pl.multiple_of(64 * k0 + g * 16, 16), 16)
                        lhs0[e, at, 256 * s0 + 128 * h : 256 * s0 + 128 * h + 128] = pair[s0].astype(BF16)
            for k in range(1, 16):
                q = [b0[k], b1[k], crot(b0[k], k, 32, 1)]
                q = [(2.0 * a, 2.0 * b) for a, b in q]
                q = [(a.astype(BF16), b.astype(BF16), (-a).astype(BF16)) for a, b in q]
                for k0 in range(2):
                    re_at = pl.ds(pl.multiple_of(64 * k0 + g * 16, 16), 16)
                    im_at = pl.ds(pl.multiple_of(128 + 64 * k0 + g * 16, 16), 16)
                    for s0 in range(2):
                        a, b, na = q[k0 + s0]
                        c0 = 512 * s0 + 128 * h
                        lhs[k - 1, re_at, c0 : c0 + 128] = a
                        lhs[k - 1, re_at, c0 + 256 : c0 + 384] = b
                        lhs[k - 1, im_at, c0 : c0 + 128] = b
                        lhs[k - 1, im_at, c0 + 256 : c0 + 384] = na
        return 0

    lax.fori_loop(0, 4, cols, 0)


def prepare_partner(p, rhs, rhs0):
    def cols(g, _):
        rows = pl.ds(pl.multiple_of(g * 16, 16), 16)
        for h in range(2):
            lanes = slice(128 * h, 128 * h + 128)
            for s0 in range(2):
                vals = [p[2 * s1 + s0, rows, lanes].astype(F32) for s1 in range(16)] + [None] * 16
                bins = rfft_bins(vals)
                for b in range(4):
                    at = pl.ds(pl.multiple_of(64 * b + g * 16, 16), 16)
                    turn = (b - 2) % 128

                    def moved(v):
                        return (pltpu.roll(v, turn, 1) if turn else v).astype(BF16)

                    for e, k in enumerate((0, 16)):
                        rhs0[e, at, 256 * s0 + 128 * h : 256 * s0 + 128 * h + 128] = moved(bins[k][0])
                    for k in range(1, 16):
                        c0 = 512 * s0 + 128 * h
                        rhs[k - 1, at, c0 : c0 + 128] = moved(bins[k][0])
                        rhs[k - 1, at, c0 + 256 : c0 + 384] = moved(bins[k][1])
        return 0

    lax.fori_loop(0, 4, cols, 0)


def multiply(lhs, lhs0, rhs, rhs0, y):
    for e, k in enumerate((0, 16)):
        y[k] = lax.dot_general(lhs0[e], rhs0[e], NT, preferred_element_type=F32).reshape(2, 64, 256)

    def one(k, _):
        d = lax.dot_general(lhs[k], rhs[k], NT, preferred_element_type=F32)
        y[k + 1] = d[:128].reshape(2, 64, 256)
        y[k + 17] = d[128:].reshape(2, 64, 256)
        return 0

    lax.fori_loop(0, 15, one, 0)


def to_lags(y, t, scale):
    def cols(g, _):
        rows = pl.ds(pl.multiple_of(g * 8, 8), 8)
        for k0 in range(2):
            for h in range(2):
                lanes = slice(128 * h, 128 * h + 128)
                bins = {}
                for k in range(17):
                    re = y[k, k0, rows, lanes]
                    im = y[k + 16, k0, rows, lanes] if 0 < k < 16 else None
                    bins[k] = (re, im)
                vals = irfft_real(bins, 32, keep_half=True)
                for k1 in range(16):
                    at = pl.ds(pl.multiple_of(64 * (2 * k1 + k0) + 8 * g, 8), 8)
                    t[h, at, :] = vals[k1] * scale
        return 0

    lax.fori_loop(0, 8, cols, 0)


def place(t, out):
    low = lax.broadcasted_iota(jnp.int32, (32, 128), 1) < 64

    def pair(g, _):
        i0 = 2 * g
        parts = []
        for h in range(2):
            u = t[h, pl.ds(i0, 32, stride=64), :]
            v = t[h, pl.ds(i0 + 1, 32, stride=64), :]
            parts.append(jnp.where(low, u, pltpu.roll(v, 64, 1)))
            parts.append(jnp.where(low, pltpu.roll(u, 64, 1), v))
        m = jnp.concatenate(parts, 0).T
        out[i0] = m[:64]
        out[i0 + 1] = m[64:]
        return 0

    lax.fori_loop(0, 32, pair, 0)


def correlate_all(own, p0, p1, p2, p3, reach, out, lhs, lhs0, rhs, rhs0, y, t, stage, sems):
    first = lax.axis_index("freq") * (OFF // 2)
    prepare_own(own, lhs, lhs0)
    copies = []
    for m, p in enumerate((p0, p1, p2, p3)):
        prepare_partner(p, rhs, rhs0)
        multiply(lhs, lhs0, rhs, rhs0, y)
        keep = jnp.where(first + m < reach[0], 0.5 / 32, 0.0).astype(F32)
        to_lags(y, t, keep)
        if m >= 2:
            copies[m - 2].wait()
        place(t, stage.at[m % 2])
        copies.append(pltpu.make_async_copy(stage.at[m % 2], out.at[m], sems.at[m % 2]))
        copies[m].start()
    copies[2].wait()
    copies[3].wait()


def per_device(blocks, traces, live, reach):
    vmem = pl.BlockSpec(memory_space=pltpu.VMEM)
    params = pltpu.CompilerParams(vmem_limit_bytes=60 * 2**20)
    tables = [jnp.asarray(a) for a in make_tables()]
    r = pl.pallas_call(
        whiten_to_time,
        out_shape=jax.ShapeDtypeStruct((32, 64, 256), BF16),
        in_specs=[vmem] * 6,
        out_specs=vmem,
        scratch_shapes=[
            pltpu.VMEM((4096, 128), F32),
            pltpu.VMEM((2, 32, 128, 128), F32),
            pltpu.VMEM((2, 16, 128, 128), F32),
            pltpu.VMEM((16, 128, 128), F32),
            pltpu.VMEM((8, 128), BF16),
        ],
        compiler_params=params,
    )(traces, live.reshape(1, 64), *tables)
    partners = []
    for m in range(OFF // 2):
        pairs = []
        for b in range(blocks):
            for half in range(2):
                q = b + half * (OFF // 2) + m
                if q < blocks:
                    pairs.append((2 * q + half, 2 * b + half))
        partners.append(lax.ppermute(r, ("fibre", "freq"), pairs))
    out = pl.pallas_call(
        correlate_all,
        out_shape=jax.ShapeDtypeStruct((OFF // 2, 64, 64, LAGS), F32),
        in_specs=[vmem] * 5 + [pl.BlockSpec(memory_space=pltpu.SMEM)],
        out_specs=pl.BlockSpec(memory_space=pl.ANY),
        scratch_shapes=[
            pltpu.VMEM((15, 256, 1024), BF16),
            pltpu.VMEM((2, 128, 512), BF16),
            pltpu.VMEM((15, 256, 1024), BF16),
            pltpu.VMEM((2, 256, 512), BF16),
            pltpu.VMEM((32, 2, 64, 256), F32),
            pltpu.VMEM((2, 2048, 128), F32),
            pltpu.VMEM((2, 64, 64, 128), F32),
            pltpu.SemaphoreType.DMA((2,)),
        ],
        compiler_params=params,
    )(r, *partners, reach)
    return out[None]


def solution(mesh):
    placed = (P(None, "fibre", None), P("fibre"), P("fibre"))
    return jax.shard_map(
        functools.partial(per_device, mesh.shape["fibre"]),
        mesh=mesh,
        in_specs=placed,
        out_specs=P("fibre", "freq", None, None, None),
        check_vma=False,
    )
```

time: 755 us -> 219 us (0.29)
  the two profiles are of different devices: /device:TPU:23 before, /device:TPU:25 now
where the time goes in v1:
time: 219 us; the launch traced here: 218 us
  waiting for transfers between devices  107 us (49%)
  Pallas kernels  94.6 us (43%)
  starting transfers between devices  16.1 us (7%)
    ppermute x4, waiting for transfers between devices, per_device(): partners.append(lax.ppermute(r, ('fibre', 'freq'), pairs))  107 us
    pallas_call x1, Pallas kernels, per_device(): pl.pallas_call(correlate_all, out_shape=jax.ShapeDtypeStruct((OFF // 2, 6...  65.9 us
    pallas_call x1, Pallas kernels, per_device(): pl.pallas_call(whiten_to_time, out_shape=jax.ShapeDtypeStruct((32, 64, 25...  28.7 us
    ppermute x4, starting transfers between devices, per_device(): partners.append(lax.ppermute(r, ('fibre', 'freq'), pairs))  16.1 us
  transfers between devices with their start and end apart: 4, of which 4 were waited for; matrix products, arithmetic and copies ran while one was open for 0% of the time, Pallas kernels for 0%

profile of v1, /device:TPU:25, one launch (start us, length us, event | category | flops | bytes accessed | tf_op | source)
XLA Modules:
  0.0 218.0 jit_solution(2141364250630372259)
XLA Ops:
  0.0 28.7 %shard_map.73.own = bf16[32,64,256]{2,1,0:T(8,128)(2,1)} custom-call(bf16[2,64,4096]{2,1,0:T(8,128)(2,1)} %x.1, s32[1,64]{1,0:T(1,128)} %bitcast.2, bf16[256,256]{1,0:T(8,128)(2,1)} %constant.8.clone.e_fwd, bf16[256,256]{1,0:T(8,128)(2,1)} %constant.9.clone.e_inv, bf16[256,128]{1,0:T(8,128)(2,1)} %constant.10.clone.e_band, f32[2,32,128]{2,1,0:T(8,128)} %constant.11.clone.twid), custom_call_target="tpu_custom_call" | custom-call | tf_op jit(solution)/shard_map/pallas_call | solution.py:390
  28.7 7.3 %collective-permute-start.3 = (bf16[32,64,256]{2,1,0:T(8,128)(2,1)}, bf16[32,64,256]{2,1,0:T(8,128)(2,1)S(1)}, u32[]{:S(2)}, u32[]{:S(2)}) collective-permute-start(bf16[32,64,256]{2,1,0:T(8,128)(2,1)} %shard_map.73.own), channel_id=1, source_target_pairs={{6,0},{15,1},{8,2},{17,3},{10,4},{19,5},{12,6},{21,7},{14,8},{23,9... | collective-permute-start | bytes 3145736 | tf_op jit(solution)/shard_map/ppermute | solution.py:412
  36.0 3.0 %collective-permute-start.2 = (bf16[32,64,256]{2,1,0:T(8,128)(2,1)}, bf16[32,64,256]{2,1,0:T(8,128)(2,1)S(1)}, u32[]{:S(2)}, u32[]{:S(2)}) collective-permute-start(bf16[32,64,256]{2,1,0:T(8,128)(2,1)} %shard_map.73.own), channel_id=1, source_target_pairs={{4,0},{13,1},{6,2},{15,3},{8,4},{17,5},{10,6},{19,7},{12,8},{21,9}... | collective-permute-start | bytes 3145736 | tf_op jit(solution)/shard_map/ppermute | solution.py:412
  39.0 3.4 %collective-permute-start.1 = (bf16[32,64,256]{2,1,0:T(8,128)(2,1)}, bf16[32,64,256]{2,1,0:T(8,128)(2,1)S(1)}, u32[]{:S(2)}, u32[]{:S(2)}) collective-permute-start(bf16[32,64,256]{2,1,0:T(8,128)(2,1)} %shard_map.73.own), channel_id=1, source_target_pairs={{2,0},{11,1},{4,2},{13,3},{6,4},{15,5},{8,6},{17,7},{10,8},{19,9},... | collective-permute-start | bytes 3145736 | tf_op jit(solution)/shard_map/ppermute | solution.py:412
  42.5 2.4 %collective-permute-start = (bf16[32,64,256]{2,1,0:T(8,128)(2,1)}, bf16[32,64,256]{2,1,0:T(8,128)(2,1)}, u32[]{:S(2)}, u32[]{:S(2)}) collective-permute-start(bf16[32,64,256]{2,1,0:T(8,128)(2,1)} %shard_map.73.own), channel_id=1, source_target_pairs={{0,0},{9,1},{2,2},{11,3},{4,4},{13,5},{6,6},{15,7},{8,8},{17,9},{1... | collective-permute-start | bytes 3145736 | tf_op jit(solution)/shard_map/ppermute | solution.py:412
  45.5 11.4 %collective-permute-done.3.p3 = bf16[32,64,256]{2,1,0:T(8,128)(2,1)S(1)} collective-permute-done((bf16[32,64,256]{2,1,0:T(8,128)(2,1)}, bf16[32,64,256]{2,1,0:T(8,128)(2,1)S(1)}, u32[]{:S(2)}, u32[]{:S(2)}) %collective-permute-start.3) | collective-permute-done | bytes 1048608 | tf_op jit(solution)/shard_map/ppermute | solution.py:412
  56.9 0.0 copy-start
  56.9 22.5 %collective-permute-done.2.p2 = bf16[32,64,256]{2,1,0:T(8,128)(2,1)S(1)} collective-permute-done((bf16[32,64,256]{2,1,0:T(8,128)(2,1)}, bf16[32,64,256]{2,1,0:T(8,128)(2,1)S(1)}, u32[]{:S(2)}, u32[]{:S(2)}) %collective-permute-start.2) | collective-permute-done | bytes 1048608 | tf_op jit(solution)/shard_map/ppermute | solution.py:412
  79.4 0.0 copy-start.1
  79.4 22.5 %collective-permute-done.1.p1 = bf16[32,64,256]{2,1,0:T(8,128)(2,1)S(1)} collective-permute-done((bf16[32,64,256]{2,1,0:T(8,128)(2,1)}, bf16[32,64,256]{2,1,0:T(8,128)(2,1)S(1)}, u32[]{:S(2)}, u32[]{:S(2)}) %collective-permute-start.1) | collective-permute-done | bytes 1048608 | tf_op jit(solution)/shard_map/ppermute | solution.py:412
  101.8 0.0 copy-start.2
  101.8 50.3 %collective-permute-done.p0 = bf16[32,64,256]{2,1,0:T(8,128)(2,1)} collective-permute-done((bf16[32,64,256]{2,1,0:T(8,128)(2,1)}, bf16[32,64,256]{2,1,0:T(8,128)(2,1)}, u32[]{:S(2)}, u32[]{:S(2)}) %collective-permute-start) | collective-permute-done | bytes 1048608 | tf_op jit(solution)/shard_map/ppermute | solution.py:412
  152.1 0.0 copy-done
  152.1 0.0 copy-done.1
  152.1 0.0 copy-done.2
  152.1 65.9 %shard_map.74 = f32[4,64,64,128]{3,2,1,0:T(8,128)} custom-call(bf16[32,64,256]{2,1,0:T(8,128)(2,1)} %shard_map.73.own, bf16[32,64,256]{2,1,0:T(8,128)(2,1)} %collective-permute-done.p0, bf16[32,64,256]{2,1,0:T(8,128)(2,1)} %copy-done.2, bf16[32,64,256]{2,1,0:T(8,128)(2,1)} %copy-done.1, bf16[32,64,256]{2,1,0:T(8,128)(2,1)} %copy-done, s32[1]{0:T(128)S(6)} %copy.8.reach), custom_call_target="tpu_custom_call" | custom-call | tf_op jit(solution)/shard_map/pallas_call | solution.py:413
Async XLA Ops:
  28.7 28.2 %collective-permute-start.3 = (bf16[32,64,256]{2,1,0:T(8,128)(2,1)}, bf16[32,64,256]{2,1,0:T(8,128)(2,1)S(1)}, u32[]{:S(2)}, u32[]{:S(2)}) collective-permute-start(bf16[32,64,256]{2,1,0:T(8,128)(2,1)} %shard_map.73.own), channel_id=1, source_target_pairs={{6,0},{15,1},{8,2},{17,3},{10,4},{19,5},{12,6},{21,7},{14,8},{23,9... | collective-permute-start | bytes 3145736 | tf_op jit(solution)/shard_map/ppermute | solution.py:412
  36.0 43.3 %collective-permute-start.2 = (bf16[32,64,256]{2,1,0:T(8,128)(2,1)}, bf16[32,64,256]{2,1,0:T(8,128)(2,1)S(1)}, u32[]{:S(2)}, u32[]{:S(2)}) collective-permute-start(bf16[32,64,256]{2,1,0:T(8,128)(2,1)} %shard_map.73.own), channel_id=1, source_target_pairs={{4,0},{13,1},{6,2},{15,3},{8,4},{17,5},{10,6},{19,7},{12,8},{21,9}... | collective-permute-start | bytes 3145736 | tf_op jit(solution)/shard_map/ppermute | solution.py:412
  39.0 62.8 %collective-permute-start.1 = (bf16[32,64,256]{2,1,0:T(8,128)(2,1)}, bf16[32,64,256]{2,1,0:T(8,128)(2,1)S(1)}, u32[]{:S(2)}, u32[]{:S(2)}) collective-permute-start(bf16[32,64,256]{2,1,0:T(8,128)(2,1)} %shard_map.73.own), channel_id=1, source_target_pairs={{2,0},{11,1},{4,2},{13,3},{6,4},{15,5},{8,6},{17,7},{10,8},{19,9},... | collective-permute-start | bytes 3145736 | tf_op jit(solution)/shard_map/ppermute | solution.py:412
  42.5 109.7 %collective-permute-start = (bf16[32,64,256]{2,1,0:T(8,128)(2,1)}, bf16[32,64,256]{2,1,0:T(8,128)(2,1)}, u32[]{:S(2)}, u32[]{:S(2)}) collective-permute-start(bf16[32,64,256]{2,1,0:T(8,128)(2,1)} %shard_map.73.own), channel_id=1, source_target_pairs={{0,0},{9,1},{2,2},{11,3},{4,4},{13,5},{6,6},{15,7},{8,8},{17,9},{1... | collective-permute-start | bytes 3145736 | tf_op jit(solution)/shard_map/ppermute | solution.py:412
  56.9 95.2 %copy-start = (bf16[32,64,256]{2,1,0:T(8,128)(2,1)}, bf16[32,64,256]{2,1,0:T(8,128)(2,1)S(1)}, u32[]{:S(2)}) copy-start(bf16[32,64,256]{2,1,0:T(8,128)(2,1)S(1)} %collective-permute-done.3.p3) | copy-start | bytes 3145732
  79.4 72.8 %copy-start.1 = (bf16[32,64,256]{2,1,0:T(8,128)(2,1)}, bf16[32,64,256]{2,1,0:T(8,128)(2,1)S(1)}, u32[]{:S(2)}) copy-start(bf16[32,64,256]{2,1,0:T(8,128)(2,1)S(1)} %collective-permute-done.2.p2) | copy-start | bytes 3145732
  101.8 50.3 %copy-start.2 = (bf16[32,64,256]{2,1,0:T(8,128)(2,1)}, bf16[32,64,256]{2,1,0:T(8,128)(2,1)S(1)}, u32[]{:S(2)}) copy-start(bf16[32,64,256]{2,1,0:T(8,128)(2,1)S(1)} %collective-permute-done.1.p1) | copy-start | bytes 3145732

commit v2 on v1

--- a/solution.py
+++ b/solution.py
@@ -149,25 +149,30 @@
     return lower + [e[i] - d[i] for i in range(half)]
 
 
-def whiten_to_time(x, live, e_fwd, e_inv, e_band, twid, r, xt, z, spec, pw, yh):
+def transpose_in(x, xt):
     def tr(q, _):
         col = pl.ds(pl.multiple_of(q * 128, 128), 128)
-        for w in range(2):
-            part = x[w, :, col].astype(F32)
-            xt[col, w * 64 : w * 64 + 64] = part.T
-        return 0
-
-    lax.fori_loop(0, 32, tr, 0)
-
-    def dft_l(s, _):
-        v = xt[pl.ds(s, 128, stride=32), :].T.astype(BF16)
+        part = jnp.concatenate([x[0, :, col], x[1, :, col]], 0)
+        xt[col] = part.T.astype(F32)
+        return 0
+
+    lax.fori_loop(0, 32, tr, 0, unroll=8)
+
+
+def dft_lanes(xt, e_fwd, z):
+    def some(q, _):
+        v = [xt[pl.ds(8 * q + k, 128, stride=32), :].T.astype(BF16) for k in range(8)]
+        v = jnp.concatenate(v, 0)
         g = jnp.dot(jnp.concatenate([v, v], 1), e_fwd[...], preferred_element_type=F32)
-        z[0, s] = g[:, :128]
-        z[1, s] = g[:, 128:]
-        return 0
-
-    lax.fori_loop(0, 32, dft_l, 0)
-
+        g = g.reshape(8, 128, 256)
+        z[0, pl.ds(8 * q, 8)] = g[:, :, :128]
+        z[1, pl.ds(8 * q, 8)] = g[:, :, 128:]
+        return 0
+
+    lax.fori_loop(0, 4, some, 0)
+
+
+def fft_steps(z, twid, spec, pw):
     def fwd(g, _):
         rows = pl.ds(pl.multiple_of(g * 8, 8), 8)
         for s0 in range(8):
@@ -194,19 +199,27 @@
 
     lax.fori_loop(0, 16, fwd, 0)
 
+
+def gains(live, e_band, pw):
     alive = jnp.concatenate([live[...], live[...]], 1).astype(F32)
     alive = jnp.broadcast_to(alive, (128, 128)).T * 2.0**-8
     lane = lax.broadcasted_iota(jnp.int32, (128, 128), 1)
 
-    def band_gain(f, _):
-        hi, lo = split_bf16(pw[f])
+    def some(q, _):
+        hi, lo = split_bf16(pw[pl.ds(8 * q, 8)].reshape(1024, 128))
         bp = jnp.dot(jnp.concatenate([hi, lo], 1), e_band[...], preferred_element_type=F32)
-        gain = lax.rsqrt(bp * (1.0 / BAND) + 1e-6) * alive
-        pw[f] = jnp.where((lane == 0) & (f == 0), gain * math.sqrt(0.5), gain)
-        return 0
-
-    lax.fori_loop(0, 16, band_gain, 0)
-
+        bp = bp.reshape(8, 128, 128)
+        for k in range(8):
+            gain = lax.rsqrt(bp[k] * (1.0 / BAND) + 1e-6) * alive
+            if k == 0:
+                gain = jnp.where((lane == 0) & (q == 0), gain * math.sqrt(0.5), gain)
+            pw[8 * q + k] = gain
+        return 0
+
+    lax.fori_loop(0, 2, some, 0)
+
+
+def ifft_steps(z, twid, spec, pw):
     def inv(g, _):
         rows = pl.ds(pl.multiple_of(g * 8, 8), 8)
         for f0 in range(4):
@@ -235,17 +248,30 @@
 
     lax.fori_loop(0, 16, inv, 0)
 
-    def idft_l(s, _):
-        both = jnp.concatenate([z[0, s], z[1, s]], 1)
+
+def idft_lanes(z, e_inv, r):
+    def some(q, _):
+        at = pl.ds(8 * q, 8)
+        both = jnp.concatenate([z[0, at].reshape(1024, 128), z[1, at].reshape(1024, 128)], 1)
         hi, lo = split_bf16(both)
-        d = jnp.dot(jnp.concatenate([hi, lo], 0), e_inv[...], preferred_element_type=F32)
-        d = d[:, :128] + d[:, 128:]
-        d = (d[:128] + d[128:]).astype(BF16)
-        r[s, :, 0:128] = d[:64]
-        r[s, :, 128:256] = d[64:]
-        return 0
-
-    lax.fori_loop(0, 32, idft_l, 0)
+        table = e_inv[...]
+        d = jnp.dot(hi, table, preferred_element_type=F32)
+        d = d + jnp.dot(lo, table, preferred_element_type=F32)
+        d = (d[:, :128] + d[:, 128:]).astype(BF16).reshape(8, 2, 64, 128)
+        r[at, :, 0:128] = d[:, 0]
+        r[at, :, 128:256] = d[:, 1]
+        return 0
+
+    lax.fori_loop(0, 4, some, 0)
+
+
+def whiten_to_time(x, live, e_fwd, e_inv, e_band, twid, r, xt, z, spec, pw):
+    transpose_in(x, xt)
+    dft_lanes(xt, e_fwd, z)
+    fft_steps(z, twid, spec, pw)
+    gains(live, e_band, pw)
+    ifft_steps(z, twid, spec, pw)
+    idft_lanes(z, e_inv, r)
 
 
 def prepare_own(r, lhs, lhs0):
@@ -317,13 +343,15 @@
     for e, k in enumerate((0, 16)):
         y[k] = lax.dot_general(lhs0[e], rhs0[e], NT, preferred_element_type=F32).reshape(2, 64, 256)
 
-    def one(k, _):
-        d = lax.dot_general(lhs[k], rhs[k], NT, preferred_element_type=F32)
-        y[k + 1] = d[:128].reshape(2, 64, 256)
-        y[k + 17] = d[128:].reshape(2, 64, 256)
-        return 0
-
-    lax.fori_loop(0, 15, one, 0)
+    def some(q, _):
+        for i in range(5):
+            k = 5 * q + i
+            d = lax.dot_general(lhs[k], rhs[k], NT, preferred_element_type=F32)
+            y[k + 1] = d[:128].reshape(2, 64, 256)
+            y[k + 17] = d[128:].reshape(2, 64, 256)
+        return 0
+
+    lax.fori_loop(0, 3, some, 0)
 
 
 def to_lags(y, t, scale):
@@ -349,73 +377,111 @@
 def place(t, out):
     low = lax.broadcasted_iota(jnp.int32, (32, 128), 1) < 64
 
-    def pair(g, _):
-        i0 = 2 * g
-        parts = []
-        for h in range(2):
-            u = t[h, pl.ds(i0, 32, stride=64), :]
-            v = t[h, pl.ds(i0 + 1, 32, stride=64), :]
-            parts.append(jnp.where(low, u, pltpu.roll(v, 64, 1)))
-            parts.append(jnp.where(low, pltpu.roll(u, 64, 1), v))
-        m = jnp.concatenate(parts, 0).T
-        out[i0] = m[:64]
-        out[i0 + 1] = m[64:]
-        return 0
-
-    lax.fori_loop(0, 32, pair, 0)
-
-
-def correlate_all(own, p0, p1, p2, p3, reach, out, lhs, lhs0, rhs, rhs0, y, t, stage, sems):
-    first = lax.axis_index("freq") * (OFF // 2)
-    prepare_own(own, lhs, lhs0)
-    copies = []
-    for m, p in enumerate((p0, p1, p2, p3)):
-        prepare_partner(p, rhs, rhs0)
+    def pairs(g, _):
+        for n in range(8):
+            i0 = 2 * (8 * g + n)
+            parts = []
+            for h in range(2):
+                u = t[h, pl.ds(i0, 32, stride=64), :]
+                v = t[h, pl.ds(i0 + 1, 32, stride=64), :]
+                parts.append(jnp.where(low, u, pltpu.roll(v, 64, 1)))
+                parts.append(jnp.where(low, pltpu.roll(u, 64, 1), v))
+            m = jnp.concatenate(parts, 0).T
+            out[i0] = m[:64]
+            out[i0 + 1] = m[64:]
+        return 0
+
+    lax.fori_loop(0, 4, pairs, 0)
+
+
+MESH = pl.DeviceIdType.MESH
+
+
+def whole(blocks, x, live, reach, e_fwd, e_inv, e_band, twid, out, xt, z, spec, pw, r, parts, lhs, lhs0, rhs, rhs0, y, t, stage, sent, got, done):
+    b = lax.axis_index("fibre")
+    half = lax.axis_index("freq")
+    first = half * (OFF // 2)
+
+    barrier = pltpu.get_barrier_semaphore()
+    greeted = 0
+    for m in range(OFF // 2):
+        step = first + m
+        for other in (b - step, b + step):
+            exists = (other >= 0) & (other < blocks) & (step > 0)
+
+            @pl.when(exists)
+            def _():
+                pl.semaphore_signal(barrier, inc=1, device_id=(other, half), device_id_type=MESH)
+
+            greeted = greeted + jnp.where(exists, 1, 0)
+
+    whiten_to_time(x, live, e_fwd, e_inv, e_band, twid, r, xt, z, spec, pw)
+    pl.semaphore_wait(barrier, greeted)
+
+    def copy(m):
+        return pltpu.make_async_remote_copy(
+            src_ref=r, dst_ref=parts.at[m], send_sem=sent.at[m], recv_sem=got.at[m],
+            device_id=(b - first - m, half), device_id_type=MESH,
+        )
+
+    for m in range(OFF // 2):
+
+        @pl.when((first + m > 0) & (b - first - m >= 0))
+        def _():
+            copy(m).start()
+
+    prepare_own(r, lhs, lhs0)
+    for m in range(OFF // 2):
+        step = first + m
+
+        @pl.when(step == 0)
+        def _():
+            parts[m] = r[...]
+
+        @pl.when((step > 0) & (b + step >= blocks))
+        def _():
+            parts[m] = jnp.zeros_like(r)
+
+        @pl.when((step > 0) & (b + step < blocks))
+        def _():
+            copy(m).wait_recv()
+
+        prepare_partner(parts.at[m], rhs, rhs0)
         multiply(lhs, lhs0, rhs, rhs0, y)
-        keep = jnp.where(first + m < reach[0], 0.5 / 32, 0.0).astype(F32)
+        keep = jnp.where(step < reach[0], 0.5 / 32, 0.0).astype(F32)
         to_lags(y, t, keep)
+
+        def store(n):
+            return pltpu.make_async_copy(stage.at[n % 2], out.at[n], done.at[n % 2])
+
         if m >= 2:
-            copies[m - 2].wait()
+            store(m - 2).wait()
         place(t, stage.at[m % 2])
-        copies.append(pltpu.make_async_copy(stage.at[m % 2], out.at[m], sems.at[m % 2]))
-        copies[m].start()
-    copies[2].wait()
-    copies[3].wait()
+        store(m).start()
+    store(2).wait()
+    store(3).wait()
+    for m in range(OFF // 2):
+
+        @pl.when((first + m > 0) & (b - first - m >= 0))
+        def _():
+            copy(m).wait_send()
 
 
 def per_device(blocks, traces, live, reach):
     vmem = pl.BlockSpec(memory_space=pltpu.VMEM)
-    params = pltpu.CompilerParams(vmem_limit_bytes=60 * 2**20)
     tables = [jnp.asarray(a) for a in make_tables()]
-    r = pl.pallas_call(
-        whiten_to_time,
-        out_shape=jax.ShapeDtypeStruct((32, 64, 256), BF16),
-        in_specs=[vmem] * 6,
-        out_specs=vmem,
+    out = pl.pallas_call(
+        functools.partial(whole, blocks),
+        out_shape=jax.ShapeDtypeStruct((OFF // 2, 64, 64, LAGS), F32),
+        in_specs=[vmem, vmem, pl.BlockSpec(memory_space=pltpu.SMEM)] + [vmem] * 4,
+        out_specs=pl.BlockSpec(memory_space=pl.ANY),
         scratch_shapes=[
             pltpu.VMEM((4096, 128), F32),
             pltpu.VMEM((2, 32, 128, 128), F32),
             pltpu.VMEM((2, 16, 128, 128), F32),
             pltpu.VMEM((16, 128, 128), F32),
-            pltpu.VMEM((8, 128), BF16),
-        ],
-        compiler_params=params,
-    )(traces, live.reshape(1, 64), *tables)
-    partners = []
-    for m in range(OFF // 2):
-        pairs = []
-        for b in range(blocks):
-            for half in range(2):
-                q = b + half * (OFF // 2) + m
-                if q < blocks:
-                    pairs.append((2 * q + half, 2 * b + half))
-        partners.append(lax.ppermute(r, ("fibre", "freq"), pairs))
-    out = pl.pallas_call(
-        correlate_all,
-        out_shape=jax.ShapeDtypeStruct((OFF // 2, 64, 64, LAGS), F32),
-        in_specs=[vmem] * 5 + [pl.BlockSpec(memory_space=pltpu.SMEM)],
-        out_specs=pl.BlockSpec(memory_space=pl.ANY),
-        scratch_shapes=[
+            pltpu.VMEM((32, 64, 256), BF16),
+            pltpu.VMEM((4, 32, 64, 256), BF16),
             pltpu.VMEM((15, 256, 1024), BF16),
             pltpu.VMEM((2, 128, 512), BF16),
             pltpu.VMEM((15, 256, 1024), BF16),
@@ -423,10 +489,14 @@
             pltpu.VMEM((32, 2, 64, 256), F32),
             pltpu.VMEM((2, 2048, 128), F32),
             pltpu.VMEM((2, 64, 64, 128), F32),
+            pltpu.SemaphoreType.DMA((4,)),
+            pltpu.SemaphoreType.DMA((4,)),
             pltpu.SemaphoreType.DMA((2,)),
         ],
-        compiler_params=params,
-    )(r, *partners, reach)
+        compiler_params=pltpu.CompilerParams(
+            vmem_limit_bytes=60 * 2**20, collective_id=0, has_side_effects=True
+        ),
+    )(traces, live.reshape(1, 64), reach, *tables)
     return out[None]
 
 

time: 219 us -> 123 us (0.56)
  the two profiles are of different devices: /device:TPU:25 before, /device:TPU:23 now
where the time goes in v2:
time: 123 us
  Pallas kernels  114 us (93%)
  local copies, waits for them, and re-layouts  8.44 us (7%)
    pallas_call x1, Pallas kernels, per_device(): pl.pallas_call(functools.partial(whole, blocks), out_shape=jax.ShapeDtype...  114 us
    unnamed x1, local copies, waits for them, and re-layouts  8.44 us

profile of v2, /device:TPU:23, one launch (start us, length us, event | category | flops | bytes accessed | tf_op | source)
XLA Modules:
  0.0 122.7 jit_solution(12999014724844946994)
XLA Ops:
  0.7 113.6 %shard_map.73 = f32[4,64,64,128]{3,2,1,0:T(8,128)} custom-call(bf16[2,64,4096]{2,1,0:T(8,128)(2,1)} %x.1, s32[1,64]{1,0:T(1,128)} %bitcast.3, s32[1]{0:T(128)S(6)} %copy.9.reach, bf16[256,256]{1,0:T(8,128)(2,1)} %constant.8.clone.e_fwd, bf16[256,256]{1,0:T(8,128)(2,1)} %constant.9.clone.e_inv, bf16[256,128]{1,0:T(8,128)(2,1)} %constant.10.clone.e_band, ...), custom_call_target="tpu_custom_call" | custom-call | tf_op jit(solution)/shard_map/pallas_call | solution.py:473
  114.3 8.4 %copy.10 = f32[1,4,64,64,128]{4,3,2,1,0:T(8,128)} copy(f32[1,4,64,64,128]{4,3,2,1,0:T(8,128)} %bitcast.2) | data formatting | bytes 16777216

commit v3 on v2

--- a/solution.py
+++ b/solution.py
@@ -367,8 +367,8 @@
                     bins[k] = (re, im)
                 vals = irfft_real(bins, 32, keep_half=True)
                 for k1 in range(16):
-                    at = pl.ds(pl.multiple_of(64 * (2 * k1 + k0) + 8 * g, 8), 8)
-                    t[h, at, :] = vals[k1] * scale
+                    at = pl.ds(pl.multiple_of(16 * (2 * k1 + k0) + 8 * (g % 2), 8), 8)
+                    t[g // 2, h, at, :] = vals[k1] * scale
         return 0
 
     lax.fori_loop(0, 8, cols, 0)
@@ -376,103 +376,164 @@
 
 def place(t, out):
     low = lax.broadcasted_iota(jnp.int32, (32, 128), 1) < 64
-
-    def pairs(g, _):
-        for n in range(8):
-            i0 = 2 * (8 * g + n)
-            parts = []
-            for h in range(2):
-                u = t[h, pl.ds(i0, 32, stride=64), :]
-                v = t[h, pl.ds(i0 + 1, 32, stride=64), :]
-                parts.append(jnp.where(low, u, pltpu.roll(v, 64, 1)))
-                parts.append(jnp.where(low, pltpu.roll(u, 64, 1), v))
-            m = jnp.concatenate(parts, 0).T
-            out[i0] = m[:64]
-            out[i0 + 1] = m[64:]
-        return 0
-
-    lax.fori_loop(0, 4, pairs, 0)
+    for i in range(0, 16, 2):
+        parts = []
+        for h in range(2):
+            u = t[0, 0, h, pl.ds(i, 32, stride=16), :]
+            v = t[0, 0, h, pl.ds(i + 1, 32, stride=16), :]
+            parts.append(jnp.where(low, u, pltpu.roll(v, 64, 1)))
+            parts.append(jnp.where(low, pltpu.roll(u, 64, 1), v))
+        m = jnp.concatenate(parts, 0).T
+        out[0, i] = m[:64]
+        out[0, i + 1] = m[64:]
 
 
 MESH = pl.DeviceIdType.MESH
 
 
-def whole(blocks, x, live, reach, e_fwd, e_inv, e_band, twid, out, xt, z, spec, pw, r, parts, lhs, lhs0, rhs, rhs0, y, t, stage, sent, got, done):
-    b = lax.axis_index("fibre")
+def whole(chips, x, live, reach, e_fwd, e_inv, e_band, twid, out, xt, z, spec, pw, parts, lhs, lhs0, rhs, rhs0, y, t, sent, got, done):
+    fibre = lax.axis_index("fibre")
     half = lax.axis_index("freq")
-    first = half * (OFF // 2)
+    c, core = fibre // 2, fibre % 2
+    column = c % 4
+    near = half == 0
+    far = half == 1
+    on_a = core == 0
+    on_b = core == 1
+    own = 4 * half
+
+    def has(k):
+        return c + k < chips
+
+    def back(k):
+        return c - k >= 0
 
     barrier = pltpu.get_barrier_semaphore()
-    greeted = 0
-    for m in range(OFF // 2):
-        step = first + m
-        for other in (b - step, b + step):
-            exists = (other >= 0) & (other < blocks) & (step > 0)
-
-            @pl.when(exists)
-            def _():
-                pl.semaphore_signal(barrier, inc=1, device_id=(other, half), device_id_type=MESH)
-
-            greeted = greeted + jnp.where(exists, 1, 0)
-
-    whiten_to_time(x, live, e_fwd, e_inv, e_band, twid, r, xt, z, spec, pw)
+    greeted = jnp.int32(0)
+
+    def greet(when, chip, its_core, its_half):
+        @pl.when(when)
+        def _():
+            pl.semaphore_signal(
+                barrier, inc=1, device_id=(2 * chip + its_core, its_half), device_id_type=MESH
+            )
+
+        return jnp.where(when, 1, 0)
+
+    for k in range(-4, 5):
+        within = (c + k >= 0) & (c + k < chips)
+        if k:
+            greeted = greeted + greet(within, c + k, core, half)
+        greeted = greeted + greet(within, c + k, 1 - core, half)
+    greeted = greeted + greet(near & on_b & back(3), c - 3, 0, 1)
+    greeted = greeted + greet(far & on_a & has(3), c + 3, 1, 0)
+
+    whiten_to_time(x, live, e_fwd, e_inv, e_band, twid, parts.at[own], xt, z, spec, pw)
     pl.semaphore_wait(barrier, greeted)
 
-    def copy(m):
+    def copy(n, src, dst, chip, its_core, its_half):
         return pltpu.make_async_remote_copy(
-            src_ref=r, dst_ref=parts.at[m], send_sem=sent.at[m], recv_sem=got.at[m],
-            device_id=(b - first - m, half), device_id_type=MESH,
+            src_ref=parts.at[src],
+            dst_ref=parts.at[dst],
+            send_sem=sent.at[n],
+            recv_sem=got.at[n],
+            device_id=(2 * chip + its_core, its_half),
+            device_id_type=MESH,
         )
 
-    for m in range(OFF // 2):
-
-        @pl.when((first + m > 0) & (b - first - m >= 0))
+    own_a1 = far & on_a & (column == 3) & back(3)
+    own_a2 = far & on_a & (column >= 2) & back(2)
+    relay_a3 = far & on_b & (column <= 2) & has(4)
+    relay_a2 = far & on_b & (column <= 1) & has(4)
+    flows = {
+        "A1": (near & on_a & back(1), copy(0, 0, 2, c - 1, 0, 0), near & on_a & has(1)),
+        "B1": (near & on_b & back(1), copy(1, 0, 2, c - 1, 1, 0), near & on_b & has(1)),
+        "A2": (near & on_a & back(2), copy(2, 0, 3, c - 2, 1, 0), near & on_b & has(2)),
+        "B0": (near & on_b, copy(3, 0, 1, c, 0, 0), near & on_a),
+        "A1s": (near & on_a & has(1), copy(4, 2, 1, c, 1, 0), near & on_b & has(1)),
+        "B1s": (near & on_b & has(1), copy(5, 2, 3, c, 0, 0), near & on_a & has(1)),
+        "fA4": (far & on_a & back(4), copy(6, 4, 3, c - 4, 1, 1), far & on_b & has(4)),
+        "fA3own": (own_a1, copy(7, 4, 1, c - 3, 1, 1), far & on_b & has(3)),
+        "fA3": (relay_a3, copy(7, 3, 1, c + 1, 1, 1), None),
+        "fA2own": (own_a2, copy(8, 4, 0, c - 2, 0, 1), far & on_a & has(2)),
+        "fA2": (relay_a2, copy(8, 3, 0, c + 2, 0, 1), None),
+        "fB2": (far & on_b & back(2), copy(9, 4, 1, c - 2, 0, 1), far & on_a & has(2)),
+        "fB3": (near & on_b & back(3), copy(10, 0, 3, c - 3, 0, 1), far & on_a & has(3)),
+        "fA3s": (far & on_b & has(3), copy(11, 1, 2, c, 0, 1), far & on_a & has(3)),
+        "fB2s": (far & on_a & has(2), copy(12, 1, 0, c, 1, 1), far & on_b & has(2)),
+        "fB3s": (far & on_a & has(3), copy(13, 3, 2, c, 1, 1), far & on_b & has(3)),
+    }
+
+    def send(name):
+        @pl.when(flows[name][0])
         def _():
-            copy(m).start()
-
-    prepare_own(r, lhs, lhs0)
-    for m in range(OFF // 2):
-        step = first + m
-
-        @pl.when(step == 0)
+            flows[name][1].start()
+
+    def receive(name):
+        @pl.when(flows[name][2])
         def _():
-            parts[m] = r[...]
-
-        @pl.when((step > 0) & (b + step >= blocks))
+            flows[name][1].wait_recv()
+
+    for name in ("fA4", "fA3own", "fA2own", "fB2", "A1", "B1", "A2", "B0", "fB3"):
+        send(name)
+
+    prepare_own(parts.at[own], lhs, lhs0)
+
+    def order(n):
+        a0, b0, a1, b1 = ((0, 0, 1, 3), (1, 2, 0, 0), (2, 1, 3, 1), (3, 3, 2, 2))[n]
+        return jnp.where(near, jnp.where(on_a, a0, b0), jnp.where(on_a, a1, b1))
+
+    def store(n):
+        return pltpu.make_async_copy(t.at[n % 2], out.at[order(n)], done.at[n % 2])
+
+    for n in range(OFF // 2):
+        if n == 0:
+            receive("fB2"), send("fB2s")
+            receive("fA4"), send("fA3"), send("fA2")
+        elif n == 1:
+            receive("B0")
+            receive("B1"), send("B1s")
+            receive("fA2own")
+            receive("fB2s")
+        elif n == 2:
+            receive("A1"), send("A1s")
+            receive("A1s")
+            receive("fB3"), send("fB3s")
+            receive("fA3own"), send("fA3s")
+        else:
+            receive("B1s")
+            receive("A2")
+            receive("fA3s")
+            receive("fB3s")
+        m = order(n)
+        step = half * (OFF // 2) + m
+
+        @pl.when(fibre + step >= 2 * chips)
         def _():
-            parts[m] = jnp.zeros_like(r)
-
-        @pl.when((step > 0) & (b + step < blocks))
-        def _():
-            copy(m).wait_recv()
+            parts[m] = jnp.zeros(parts.shape[1:], parts.dtype)
 
         prepare_partner(parts.at[m], rhs, rhs0)
         multiply(lhs, lhs0, rhs, rhs0, y)
         keep = jnp.where(step < reach[0], 0.5 / 32, 0.0).astype(F32)
-        to_lags(y, t, keep)
-
-        def store(n):
-            return pltpu.make_async_copy(stage.at[n % 2], out.at[n], done.at[n % 2])
-
-        if m >= 2:
-            store(m - 2).wait()
-        place(t, stage.at[m % 2])
-        store(m).start()
+        if n >= 2:
+            store(n - 2).wait()
+        to_lags(y, t.at[n % 2], keep)
+        store(n).start()
     store(2).wait()
     store(3).wait()
-    for m in range(OFF // 2):
-
-        @pl.when((first + m > 0) & (b - first - m >= 0))
+    for name in flows:
+
+        @pl.when(flows[name][0])
         def _():
-            copy(m).wait_send()
-
-
-def per_device(blocks, traces, live, reach):
+            flows[name][1].wait_send()
+
+
+def per_device(chips, traces, live, reach):
     vmem = pl.BlockSpec(memory_space=pltpu.VMEM)
     tables = [jnp.asarray(a) for a in make_tables()]
-    out = pl.pallas_call(
-        functools.partial(whole, blocks),
-        out_shape=jax.ShapeDtypeStruct((OFF // 2, 64, 64, LAGS), F32),
+    lags = pl.pallas_call(
+        functools.partial(whole, chips),
+        out_shape=jax.ShapeDtypeStruct((OFF // 2, 4, 2, 512, 128), F32),
         in_specs=[vmem, vmem, pl.BlockSpec(memory_space=pltpu.SMEM)] + [vmem] * 4,
         out_specs=pl.BlockSpec(memory_space=pl.ANY),
         scratch_shapes=[
@@ -480,30 +541,35 @@
             pltpu.VMEM((2, 32, 128, 128), F32),
             pltpu.VMEM((2, 16, 128, 128), F32),
             pltpu.VMEM((16, 128, 128), F32),
-            pltpu.VMEM((32, 64, 256), BF16),
-            pltpu.VMEM((4, 32, 64, 256), BF16),
+            pltpu.VMEM((5, 32, 64, 256), BF16),
             pltpu.VMEM((15, 256, 1024), BF16),
             pltpu.VMEM((2, 128, 512), BF16),
             pltpu.VMEM((15, 256, 1024), BF16),
             pltpu.VMEM((2, 256, 512), BF16),
             pltpu.VMEM((32, 2, 64, 256), F32),
-            pltpu.VMEM((2, 2048, 128), F32),
-            pltpu.VMEM((2, 64, 64, 128), F32),
-            pltpu.SemaphoreType.DMA((4,)),
-            pltpu.SemaphoreType.DMA((4,)),
+            pltpu.VMEM((2, 4, 2, 512, 128), F32),
+            pltpu.SemaphoreType.DMA((14,)),
+            pltpu.SemaphoreType.DMA((14,)),
             pltpu.SemaphoreType.DMA((2,)),
         ],
         compiler_params=pltpu.CompilerParams(
             vmem_limit_bytes=60 * 2**20, collective_id=0, has_side_effects=True
         ),
     )(traces, live.reshape(1, 64), reach, *tables)
+    out = pl.pallas_call(
+        place,
+        out_shape=jax.ShapeDtypeStruct((OFF // 2, 64, 64, LAGS), F32),
+        grid=(OFF // 2, 4),
+        in_specs=[pl.BlockSpec((1, 1, 2, 512, 128), lambda m, q: (m, q, 0, 0, 0))],
+        out_specs=pl.BlockSpec((1, 16, 64, LAGS), lambda m, q: (m, q, 0, 0)),
+    )(lags)
     return out[None]
 
 
 def solution(mesh):
     placed = (P(None, "fibre", None), P("fibre"), P("fibre"))
     return jax.shard_map(
-        functools.partial(per_device, mesh.shape["fibre"]),
+        functools.partial(per_device, mesh.shape["fibre"] // 2),
         mesh=mesh,
         in_specs=placed,
         out_specs=P("fibre", "freq", None, None, None),

time: 123 us -> 91.5 us (0.74)
  Pallas kernels: 114 us -> 89.6 us
  local copies, waits for them, and re-layouts: 8.44 us -> 0 us
    pallas_call x1 -> x2, Pallas kernels: 114 us -> 89.6 us  [the longest x1 75.2 us: per_device(): pl.pallas_call(functools.partial(whole, chips), out_shape=jax.ShapeDtypeS...]
    unnamed x1 -> x0, local copies, waits for them, and re-layouts: 8.44 us -> none
where the time goes in v3:
time: 91.5 us; the launch traced here: 90.2 us
  Pallas kernels  89.6 us (98%)
    pallas_call x1, Pallas kernels, per_device(): pl.pallas_call(functools.partial(whole, chips), out_shape=jax.ShapeDtypeS...  75.2 us
    pallas_call x1, Pallas kernels, per_device(): pl.pallas_call(place, out_shape=jax.ShapeDtypeStruct((OFF // 2, 64, 64, L...  14.4 us

profile of v3, /device:TPU:23, one launch (start us, length us, event | category | flops | bytes accessed | tf_op | source)
XLA Modules:
  0.0 90.2 jit_solution(15157827090839724405)
XLA Ops:
  0.7 75.2 %shard_map.73.t = f32[4,4,2,512,128]{4,3,2,1,0:T(8,128)} custom-call(bf16[2,64,4096]{2,1,0:T(8,128)(2,1)} %x.1, s32[1,64]{1,0:T(1,128)} %bitcast.2, s32[1]{0:T(128)S(6)} %copy.8.reach, bf16[256,256]{1,0:T(8,128)(2,1)} %constant.8.clone.e_fwd, bf16[256,256]{1,0:T(8,128)(2,1)} %constant.9.clone.e_inv, bf16[256,128]{1,0:T(8,128)(2,1)} %constant.10.clone.e_band, ...), custom_call_target="tpu_custom_call" | custom-call | tf_op jit(solution)/shard_map/pallas_call | solution.py:534
  75.8 14.4 %shard_map.74 = f32[4,64,64,128]{3,2,1,0:T(8,128)} custom-call(f32[4,4,2,512,128]{4,3,2,1,0:T(8,128)} %shard_map.73.t), custom_call_target="tpu_custom_call" | custom-call | tf_op jit(solution)/shard_map/pallas_call | solution.py:559

commit v4 on v3

--- a/solution.py
+++ b/solution.py
@@ -265,9 +265,12 @@
     lax.fori_loop(0, 4, some, 0)
 
 
-def whiten_to_time(x, live, e_fwd, e_inv, e_band, twid, r, xt, z, spec, pw):
+def whiten_begin(x, e_fwd, xt, z):
     transpose_in(x, xt)
     dft_lanes(xt, e_fwd, z)
+
+
+def whiten_end(live, e_inv, e_band, twid, r, z, spec, pw):
     fft_steps(z, twid, spec, pw)
     gains(live, e_band, pw)
     ifft_steps(z, twid, spec, pw)
@@ -281,33 +284,20 @@
             lanes = slice(128 * h, 128 * h + 128)
             spectra = []
             for n0 in range(2):
-                vals = []
-                for n1 in range(16):
-                    vals.append(r[2 * n1 + n0, rows, lanes].astype(F32))
+                vals = [r[2 * n1 + n0, rows, lanes].astype(F32) for n1 in range(16)]
                 vals += [pltpu.roll(v, 127, 1) for v in vals]
                 spectra.append(rfft_bins(vals))
             b0, b1 = spectra
             for e, k in enumerate((0, 16)):
-                sgn = 1.0 if k == 0 else -1.0
-                q0, q1, q2 = b0[k][0], b1[k][0], b0[k][0] * sgn
-                for k0, pair in enumerate(((q0, q1), (q1, q2))):
-                    for s0 in range(2):
-                        at = pl.ds(pl.multiple_of(64 * k0 + g * 16, 16), 16)
-                        lhs0[e, at, 256 * s0 + 128 * h : 256 * s0 + 128 * h + 128] = pair[s0].astype(BF16)
+                last = b0[k][0] if k == 0 else -b0[k][0]
+                for n0, v in enumerate((b0[k][0], b1[k][0], last)):
+                    lhs0[e, n0, rows, lanes] = v.astype(BF16)
             for k in range(1, 16):
-                q = [b0[k], b1[k], crot(b0[k], k, 32, 1)]
-                q = [(2.0 * a, 2.0 * b) for a, b in q]
-                q = [(a.astype(BF16), b.astype(BF16), (-a).astype(BF16)) for a, b in q]
-                for k0 in range(2):
-                    re_at = pl.ds(pl.multiple_of(64 * k0 + g * 16, 16), 16)
-                    im_at = pl.ds(pl.multiple_of(128 + 64 * k0 + g * 16, 16), 16)
-                    for s0 in range(2):
-                        a, b, na = q[k0 + s0]
-                        c0 = 512 * s0 + 128 * h
-                        lhs[k - 1, re_at, c0 : c0 + 128] = a
-                        lhs[k - 1, re_at, c0 + 256 : c0 + 384] = b
-                        lhs[k - 1, im_at, c0 : c0 + 128] = b
-                        lhs[k - 1, im_at, c0 + 256 : c0 + 384] = na
+                for n0, v in enumerate((b0[k], b1[k], crot(b0[k], k, 32, 1))):
+                    re, im = (2.0 * v[0]).astype(BF16), (2.0 * v[1]).astype(BF16)
+                    lhs[k - 1, 3 * n0, rows, lanes] = re
+                    lhs[k - 1, 3 * n0 + 1, rows, lanes] = im
+                    lhs[k - 1, 3 * n0 + 2, rows, lanes] = -re
         return 0
 
     lax.fori_loop(0, 4, cols, 0)
@@ -321,37 +311,41 @@
             for s0 in range(2):
                 vals = [p[2 * s1 + s0, rows, lanes].astype(F32) for s1 in range(16)] + [None] * 16
                 bins = rfft_bins(vals)
-                for b in range(4):
-                    at = pl.ds(pl.multiple_of(64 * b + g * 16, 16), 16)
-                    turn = (b - 2) % 128
-
-                    def moved(v):
-                        return (pltpu.roll(v, turn, 1) if turn else v).astype(BF16)
-
-                    for e, k in enumerate((0, 16)):
-                        rhs0[e, at, 256 * s0 + 128 * h : 256 * s0 + 128 * h + 128] = moved(bins[k][0])
-                    for k in range(1, 16):
-                        c0 = 512 * s0 + 128 * h
-                        rhs[k - 1, at, c0 : c0 + 128] = moved(bins[k][0])
-                        rhs[k - 1, at, c0 + 256 : c0 + 384] = moved(bins[k][1])
+                c0 = 256 * s0 + 128 * h
+                for e, k in enumerate((0, 16)):
+                    rhs0[e, rows, c0 : c0 + 128] = bins[k][0].astype(BF16)
+                c0 = 512 * s0 + 128 * h
+                for k in range(1, 16):
+                    rhs[k - 1, rows, c0 : c0 + 128] = bins[k][0].astype(BF16)
+                    rhs[k - 1, rows, c0 + 256 : c0 + 384] = bins[k][1].astype(BF16)
         return 0
 
     lax.fori_loop(0, 4, cols, 0)
 
 
+def turned(v):
+    tiles = [v[:, i : i + 128] for i in range(0, v.shape[1], 128)]
+    rows = []
+    for b in range(4):
+        rows.append(v if b == 2 else jnp.concatenate([pltpu.roll(a, (b - 2) % 128, 1) for a in tiles], 1))
+    return jnp.concatenate(rows, 0)
+
+
 def multiply(lhs, lhs0, rhs, rhs0, y):
+    def product(quads, partner):
+        a = jnp.concatenate([jnp.concatenate(q, 1) for q in quads], 0)
+        return lax.dot_general(a, turned(partner), NT, preferred_element_type=F32)
+
     for e, k in enumerate((0, 16)):
-        y[k] = lax.dot_general(lhs0[e], rhs0[e], NT, preferred_element_type=F32).reshape(2, 64, 256)
-
-    def some(q, _):
-        for i in range(5):
-            k = 5 * q + i
-            d = lax.dot_general(lhs[k], rhs[k], NT, preferred_element_type=F32)
-            y[k + 1] = d[:128].reshape(2, 64, 256)
-            y[k + 17] = d[128:].reshape(2, 64, 256)
-        return 0
-
-    lax.fori_loop(0, 3, some, 0)
+        a = [lhs0[e, n0] for n0 in range(3)]
+        y[k] = product((a[:2], a[1:]), rhs0[e]).reshape(2, 64, 256)
+    for k in range(15):
+        re, im, neg = ([lhs[k, 3 * n0 + c] for n0 in range(3)] for c in range(3))
+        quads = [(re[n], im[n], re[n + 1], im[n + 1]) for n in range(2)]
+        quads += [(im[n], neg[n], im[n + 1], neg[n + 1]) for n in range(2)]
+        d = product(quads, rhs[k])
+        y[k + 1] = d[:128].reshape(2, 64, 256)
+        y[k + 17] = d[128:].reshape(2, 64, 256)
 
 
 def to_lags(y, t, scale):
@@ -376,22 +370,23 @@
 
 def place(t, out):
     low = lax.broadcasted_iota(jnp.int32, (32, 128), 1) < 64
-    for i in range(0, 16, 2):
-        parts = []
-        for h in range(2):
-            u = t[0, 0, h, pl.ds(i, 32, stride=16), :]
-            v = t[0, 0, h, pl.ds(i + 1, 32, stride=16), :]
-            parts.append(jnp.where(low, u, pltpu.roll(v, 64, 1)))
-            parts.append(jnp.where(low, pltpu.roll(u, 64, 1), v))
-        m = jnp.concatenate(parts, 0).T
-        out[0, i] = m[:64]
-        out[0, i + 1] = m[64:]
+    for q in range(4):
+        for i in range(0, 16, 2):
+            parts = []
+            for h in range(2):
+                u = t[0, q, h, pl.ds(i, 32, stride=16), :]
+                v = t[0, q, h, pl.ds(i + 1, 32, stride=16), :]
+                parts.append(jnp.where(low, u, pltpu.roll(v, 64, 1)))
+                parts.append(jnp.where(low, pltpu.roll(u, 64, 1), v))
+            m = jnp.concatenate(parts, 0).T
+            out[0, 16 * q + i] = m[:64]
+            out[0, 16 * q + i + 1] = m[64:]
 
 
 MESH = pl.DeviceIdType.MESH
 
 
-def whole(chips, x, live, reach, e_fwd, e_inv, e_band, twid, out, xt, z, spec, pw, parts, lhs, lhs0, rhs, rhs0, y, t, sent, got, done):
+def whole(chips, x, live, reach, e_fwd, e_inv, e_band, twid, out, xt, z, spec, pw, x_far, live_far, parts, lhs, lhs0, rhs, rhs0, y, t, sent, got, done):
     fibre = lax.axis_index("fibre")
     half = lax.axis_index("freq")
     c, core = fibre // 2, fibre % 2
@@ -428,13 +423,13 @@
     greeted = greeted + greet(near & on_b & back(3), c - 3, 0, 1)
     greeted = greeted + greet(far & on_a & has(3), c + 3, 1, 0)
 
-    whiten_to_time(x, live, e_fwd, e_inv, e_band, twid, parts.at[own], xt, z, spec, pw)
+    whiten_begin(x, e_fwd, xt, z)
     pl.semaphore_wait(barrier, greeted)
 
     def copy(n, src, dst, chip, its_core, its_half):
         return pltpu.make_async_remote_copy(
-            src_ref=parts.at[src],
-            dst_ref=parts.at[dst],
+            src_ref=parts.at[src] if isinstance(src, (int, jax.Array)) else src,
+            dst_ref=parts.at[dst] if isinstance(dst, (int, jax.Array)) else dst,
             send_sem=sent.at[n],
             recv_sem=got.at[n],
             device_id=(2 * chip + its_core, its_half),
@@ -446,13 +441,14 @@
     relay_a3 = far & on_b & (column <= 2) & has(4)
     relay_a2 = far & on_b & (column <= 1) & has(4)
     flows = {
-        "A1": (near & on_a & back(1), copy(0, 0, 2, c - 1, 0, 0), near & on_a & has(1)),
+        "A1": (near & on_a & back(1), copy(0, 0, 1, c - 1, 1, 0), near & on_b & has(1)),
         "B1": (near & on_b & back(1), copy(1, 0, 2, c - 1, 1, 0), near & on_b & has(1)),
         "A2": (near & on_a & back(2), copy(2, 0, 3, c - 2, 1, 0), near & on_b & has(2)),
         "B0": (near & on_b, copy(3, 0, 1, c, 0, 0), near & on_a),
-        "A1s": (near & on_a & has(1), copy(4, 2, 1, c, 1, 0), near & on_b & has(1)),
+        "A1s": (near & on_b & has(1), copy(4, 1, 2, c, 0, 0), near & on_a & has(1)),
         "B1s": (near & on_b & has(1), copy(5, 2, 3, c, 0, 0), near & on_a & has(1)),
-        "fA4": (far & on_a & back(4), copy(6, 4, 3, c - 4, 1, 1), far & on_b & has(4)),
+        "fX4": (far & on_a & back(4), copy(6, x, x_far, c - 4, 1, 1), far & on_b & has(4)),
+        "fL4": (far & on_a & back(4), copy(14, live, live_far, c - 4, 1, 1), far & on_b & has(4)),
         "fA3own": (own_a1, copy(7, 4, 1, c - 3, 1, 1), far & on_b & has(3)),
         "fA3": (relay_a3, copy(7, 3, 1, c + 1, 1, 1), None),
         "fA2own": (own_a2, copy(8, 4, 0, c - 2, 0, 1), far & on_a & has(2)),
@@ -464,23 +460,42 @@
         "fB3s": (far & on_a & has(3), copy(13, 3, 2, c, 1, 1), far & on_b & has(3)),
     }
 
-    def send(name):
-        @pl.when(flows[name][0])
+    def send_if(name, when):
+        @pl.when(flows[name][0] & when)
         def _():
             flows[name][1].start()
 
-    def receive(name):
-        @pl.when(flows[name][2])
+    def receive_if(name, when):
+        @pl.when(flows[name][2] & when)
         def _():
             flows[name][1].wait_recv()
 
-    for name in ("fA4", "fA3own", "fA2own", "fB2", "A1", "B1", "A2", "B0", "fB3"):
+    def send(name):
+        send_if(name, True)
+
+    def receive(name):
+        receive_if(name, True)
+
+    send("fX4"), send("fL4")
+    whiten_end(live, e_inv, e_band, twid, parts.at[own], z, spec, pw)
+    for name in ("fA3own", "fA2own", "fB2", "fB3", "A1", "B0"):
         send(name)
 
     prepare_own(parts.at[own], lhs, lhs0)
 
+    receive("fX4"), receive("fL4")
+
+    @pl.when(far & on_b & has(4))
+    def _():
+        whiten_begin(x_far, e_fwd, xt, z)
+        whiten_end(live_far, e_inv, e_band, twid, parts.at[3], z, spec, pw)
+
+    send("fA2"), send("fA3")
+
     def order(n):
-        a0, b0, a1, b1 = ((0, 0, 1, 3), (1, 2, 0, 0), (2, 1, 3, 1), (3, 3, 2, 2))[n]
+        a0, b0, a1, b1 = ((0, 0, 1, 3), (1, 1, 0, 0), (2, 2, 3, 1), (3, 3, 2, 2))[n]
+        if n in (1, 2):
+            a1 = jnp.where(column >= 2, (0, 3, 0)[n], a1)
         return jnp.where(near, jnp.where(on_a, a0, b0), jnp.where(on_a, a1, b1))
 
     def store(n):
@@ -489,16 +504,18 @@
     for n in range(OFF // 2):
         if n == 0:
             receive("fB2"), send("fB2s")
-            receive("fA4"), send("fA3"), send("fA2")
         elif n == 1:
+            send("B1"), send("A2")
             receive("B0")
-            receive("B1"), send("B1s")
-            receive("fA2own")
+            receive("A1"), send("A1s")
+            receive_if("fA2own", column < 2)
+            receive_if("fB3", column >= 2), send_if("fB3s", column >= 2)
             receive("fB2s")
         elif n == 2:
-            receive("A1"), send("A1s")
+            receive("B1"), send("B1s")
             receive("A1s")
-            receive("fB3"), send("fB3s")
+            receive_if("fB3", column < 2), send_if("fB3s", column < 2)
+            receive_if("fA2own", column >= 2)
             receive("fA3own"), send("fA3s")
         else:
             receive("B1s")
@@ -541,15 +558,17 @@
             pltpu.VMEM((2, 32, 128, 128), F32),
             pltpu.VMEM((2, 16, 128, 128), F32),
             pltpu.VMEM((16, 128, 128), F32),
+            pltpu.VMEM((2, 64, 4096), BF16),
+            pltpu.VMEM((1, 64), jnp.int32),
             pltpu.VMEM((5, 32, 64, 256), BF16),
-            pltpu.VMEM((15, 256, 1024), BF16),
-            pltpu.VMEM((2, 128, 512), BF16),
-            pltpu.VMEM((15, 256, 1024), BF16),
-            pltpu.VMEM((2, 256, 512), BF16),
+            pltpu.VMEM((15, 9, 64, 256), BF16),
+            pltpu.VMEM((2, 3, 64, 256), BF16),
+            pltpu.VMEM((15, 64, 1024), BF16),
+            pltpu.VMEM((2, 64, 512), BF16),
             pltpu.VMEM((32, 2, 64, 256), F32),
             pltpu.VMEM((2, 4, 2, 512, 128), F32),
-            pltpu.SemaphoreType.DMA((14,)),
-            pltpu.SemaphoreType.DMA((14,)),
+            pltpu.SemaphoreType.DMA((15,)),
+            pltpu.SemaphoreType.DMA((15,)),
             pltpu.SemaphoreType.DMA((2,)),
         ],
         compiler_params=pltpu.CompilerParams(
@@ -559,9 +578,9 @@
     out = pl.pallas_call(
         place,
         out_shape=jax.ShapeDtypeStruct((OFF // 2, 64, 64, LAGS), F32),
-        grid=(OFF // 2, 4),
-        in_specs=[pl.BlockSpec((1, 1, 2, 512, 128), lambda m, q: (m, q, 0, 0, 0))],
-        out_specs=pl.BlockSpec((1, 16, 64, LAGS), lambda m, q: (m, q, 0, 0)),
+        grid=(OFF // 2,),
+        in_specs=[pl.BlockSpec((1, 4, 2, 512, 128), lambda m: (m, 0, 0, 0, 0))],
+        out_specs=pl.BlockSpec((1, 64, 64, LAGS), lambda m: (m, 0, 0, 0)),
     )(lags)
     return out[None]
 

time: 91.5 us -> 84.2 us (0.920)
  Pallas kernels: 89.6 us -> 83.2 us
    pallas_call x1, Pallas kernels: 14.4 us -> 9.29 us  [per_device(): pl.pallas_call(place, out_shape=jax.ShapeDtypeStruct((OFF // 2, 64, 64, L...]
    pallas_call x1, Pallas kernels: 75.2 us -> 73.9 us  [per_device(): pl.pallas_call(functools.partial(whole, chips), out_shape=jax.ShapeDtypeS...]
where the time goes in v4:
time: 84.2 us; the launch traced here: 83.8 us
  Pallas kernels  83.2 us (99%)
    pallas_call x1, Pallas kernels, per_device(): pl.pallas_call(functools.partial(whole, chips), out_shape=jax.ShapeDtypeS...  73.9 us
    pallas_call x1, Pallas kernels, per_device(): pl.pallas_call(place, out_shape=jax.ShapeDtypeStruct((OFF // 2, 64, 64, L...  9.29 us

profile of v4, /device:TPU:23, one launch (start us, length us, event | category | flops | bytes accessed | tf_op | source)
XLA Modules:
  0.0 83.8 jit_solution(9557235852792800666)
XLA Ops:
  0.7 73.9 %shard_map.73.t = f32[4,4,2,512,128]{4,3,2,1,0:T(8,128)} custom-call(bf16[2,64,4096]{2,1,0:T(8,128)(2,1)} %x.1, s32[1,64]{1,0:T(1,128)} %bitcast.2, s32[1]{0:T(128)S(6)} %copy.8.reach, bf16[256,256]{1,0:T(8,128)(2,1)} %constant.8.clone.e_fwd, bf16[256,256]{1,0:T(8,128)(2,1)} %constant.9.clone.e_inv, bf16[256,128]{1,0:T(8,128)(2,1)} %constant.10.clone.e_band, ...), custom_call_target="tpu_custom_call" | custom-call | tf_op jit(solution)/shard_map/pallas_call | solution.py:551
  74.5 9.3 %shard_map.74 = f32[4,64,64,128]{3,2,1,0:T(8,128)} custom-call(f32[4,4,2,512,128]{4,3,2,1,0:T(8,128)} %shard_map.73.t), custom_call_target="tpu_custom_call" | custom-call | tf_op jit(solution)/shard_map/pallas_call | solution.py:578

commit v5 on v4

--- a/solution.py
+++ b/solution.py
@@ -460,42 +460,34 @@
         "fB3s": (far & on_a & has(3), copy(13, 3, 2, c, 1, 1), far & on_b & has(3)),
     }
 
-    def send_if(name, when):
-        @pl.when(flows[name][0] & when)
+    def send(name):
+        @pl.when(flows[name][0])
         def _():
             flows[name][1].start()
 
-    def receive_if(name, when):
-        @pl.when(flows[name][2] & when)
+    def receive(name):
+        @pl.when(flows[name][2])
         def _():
             flows[name][1].wait_recv()
 
-    def send(name):
-        send_if(name, True)
-
-    def receive(name):
-        receive_if(name, True)
-
     send("fX4"), send("fL4")
     whiten_end(live, e_inv, e_band, twid, parts.at[own], z, spec, pw)
-    for name in ("fA3own", "fA2own", "fB2", "fB3", "A1", "B0"):
+    for name in ("fA3own", "fA2own", "A1", "B0"):
         send(name)
 
-    prepare_own(parts.at[own], lhs, lhs0)
-
     receive("fX4"), receive("fL4")
+    send("fB2")
 
     @pl.when(far & on_b & has(4))
     def _():
         whiten_begin(x_far, e_fwd, xt, z)
         whiten_end(live_far, e_inv, e_band, twid, parts.at[3], z, spec, pw)
 
-    send("fA2"), send("fA3")
+    send("fA3"), send("fA2")
+    prepare_own(parts.at[own], lhs, lhs0)
 
     def order(n):
-        a0, b0, a1, b1 = ((0, 0, 1, 3), (1, 1, 0, 0), (2, 2, 3, 1), (3, 3, 2, 2))[n]
-        if n in (1, 2):
-            a1 = jnp.where(column >= 2, (0, 3, 0)[n], a1)
+        a0, b0, a1, b1 = ((0, 0, 1, 3), (1, 1, 3, 0), (2, 2, 2, 2), (3, 3, 0, 1))[n]
         return jnp.where(near, jnp.where(on_a, a0, b0), jnp.where(on_a, a1, b1))
 
     def store(n):
@@ -508,20 +500,19 @@
             send("B1"), send("A2")
             receive("B0")
             receive("A1"), send("A1s")
-            receive_if("fA2own", column < 2)
-            receive_if("fB3", column >= 2), send_if("fB3s", column >= 2)
+            receive("fB3"), send("fB3s")
             receive("fB2s")
         elif n == 2:
+            send("fB3")
             receive("B1"), send("B1s")
             receive("A1s")
-            receive_if("fB3", column < 2), send_if("fB3s", column < 2)
-            receive_if("fA2own", column >= 2)
             receive("fA3own"), send("fA3s")
+            receive("fA3s")
+            receive("fB3s")
         else:
             receive("B1s")
             receive("A2")
-            receive("fA3s")
-            receive("fB3s")
+            receive("fA2own")
         m = order(n)
         step = half * (OFF // 2) + m
 

time: 84.2 us -> 77.3 us (0.918)
  the two profiles are of different devices: /device:TPU:23 before, /device:TPU:112 now
where the time goes in v5:
time: 77.3 us; the launch traced here: 77.1 us
  Pallas kernels  76.5 us (99%)
    pallas_call x1, Pallas kernels, per_device(): pl.pallas_call(functools.partial(whole, chips), out_shape=jax.ShapeDtypeS...  67.2 us
    pallas_call x1, Pallas kernels, per_device(): pl.pallas_call(place, out_shape=jax.ShapeDtypeStruct((OFF // 2, 64, 64, L...  9.29 us

profile of v5, /device:TPU:112, one launch (start us, length us, event | category | flops | bytes accessed | tf_op | source)
XLA Modules:
  0.0 77.1 jit_solution(8657017133682558287)
XLA Ops:
  0.7 67.2 %shard_map.73.t = f32[4,4,2,512,128]{4,3,2,1,0:T(8,128)} custom-call(bf16[2,64,4096]{2,1,0:T(8,128)(2,1)} %x.1, s32[1,64]{1,0:T(1,128)} %bitcast.2, s32[1]{0:T(128)S(6)} %copy.8.reach, bf16[256,256]{1,0:T(8,128)(2,1)} %constant.8.clone.e_fwd, bf16[256,256]{1,0:T(8,128)(2,1)} %constant.9.clone.e_inv, bf16[256,128]{1,0:T(8,128)(2,1)} %constant.10.clone.e_band, ...), custom_call_target="tpu_custom_call" | custom-call | tf_op jit(solution)/shard_map/pallas_call | solution.py:542
  67.9 9.3 %shard_map.74 = f32[4,64,64,128]{3,2,1,0:T(8,128)} custom-call(f32[4,4,2,512,128]{4,3,2,1,0:T(8,128)} %shard_map.73.t), custom_call_target="tpu_custom_call" | custom-call | tf_op jit(solution)/shard_map/pallas_call | solution.py:569

commit v6 on v5

--- a/solution.py
+++ b/solution.py
@@ -453,8 +453,10 @@
         "fA3": (relay_a3, copy(7, 3, 1, c + 1, 1, 1), None),
         "fA2own": (own_a2, copy(8, 4, 0, c - 2, 0, 1), far & on_a & has(2)),
         "fA2": (relay_a2, copy(8, 3, 0, c + 2, 0, 1), None),
-        "fB2": (far & on_b & back(2), copy(9, 4, 1, c - 2, 0, 1), far & on_a & has(2)),
-        "fB3": (near & on_b & back(3), copy(10, 0, 3, c - 3, 0, 1), far & on_a & has(3)),
+        "fB2": (far & on_b & back(2) & (column < 2), copy(9, 4, 1, c - 2, 0, 1), far & on_a & has(2)),
+        "fB2row": (far & on_b & (column >= 2), copy(9, 4, 1, c - 2, 0, 1), None),
+        "fB3": (near & on_b & back(3) & (column < 3), copy(10, 0, 3, c - 3, 0, 1), far & on_a & has(3)),
+        "fB3row": (near & on_b & (column == 3), copy(10, 0, 3, c - 3, 0, 1), None),
         "fA3s": (far & on_b & has(3), copy(11, 1, 2, c, 0, 1), far & on_a & has(3)),
         "fB2s": (far & on_a & has(2), copy(12, 1, 0, c, 1, 1), far & on_b & has(2)),
         "fB3s": (far & on_a & has(3), copy(13, 3, 2, c, 1, 1), far & on_b & has(3)),
@@ -472,7 +474,7 @@
 
     send("fX4"), send("fL4")
     whiten_end(live, e_inv, e_band, twid, parts.at[own], z, spec, pw)
-    for name in ("fA3own", "fA2own", "A1", "B0"):
+    for name in ("fB2row", "fA3own", "fA2own", "A1", "B0"):
         send(name)
 
     receive("fX4"), receive("fL4")
@@ -497,7 +499,7 @@
         if n == 0:
             receive("fB2"), send("fB2s")
         elif n == 1:
-            send("B1"), send("A2")
+            send("B1"), send("A2"), send("fB3row")
             receive("B0")
             receive("A1"), send("A1s")
             receive("fB3"), send("fB3s")

time: 77.3 us -> 74.8 us (0.968)
  the two profiles are of different devices: /device:TPU:112 before, /device:TPU:62 now
where the time goes in v6:
time: 74.8 us; the launch traced here: 74.6 us
  Pallas kernels  73.9 us (99%)
    pallas_call x1, Pallas kernels, per_device(): pl.pallas_call(functools.partial(whole, chips), out_shape=jax.ShapeDtypeS...  64.6 us
    pallas_call x1, Pallas kernels, per_device(): pl.pallas_call(place, out_shape=jax.ShapeDtypeStruct((OFF // 2, 64, 64, L...  9.29 us

profile of v6, /device:TPU:62, one launch (start us, length us, event | category | flops | bytes accessed | tf_op | source)
XLA Modules:
  0.0 74.6 jit_solution(6978812131198824503)
XLA Ops:
  0.7 64.6 %shard_map.73.t = f32[4,4,2,512,128]{4,3,2,1,0:T(8,128)} custom-call(bf16[2,64,4096]{2,1,0:T(8,128)(2,1)} %x.1, s32[1,64]{1,0:T(1,128)} %bitcast.2, s32[1]{0:T(128)S(6)} %copy.8.reach, bf16[256,256]{1,0:T(8,128)(2,1)} %constant.8.clone.e_fwd, bf16[256,256]{1,0:T(8,128)(2,1)} %constant.9.clone.e_inv, bf16[256,128]{1,0:T(8,128)(2,1)} %constant.10.clone.e_band, ...), custom_call_target="tpu_custom_call" | custom-call | tf_op jit(solution)/shard_map/pallas_call | solution.py:544
  65.3 9.3 %shard_map.74 = f32[4,64,64,128]{3,2,1,0:T(8,128)} custom-call(f32[4,4,2,512,128]{4,3,2,1,0:T(8,128)} %shard_map.73.t), custom_call_target="tpu_custom_call" | custom-call | tf_op jit(solution)/shard_map/pallas_call | solution.py:571
